TPU v7x, 32 devices: a whole 2x2x4 slice. The times are simulated.
32 devices in a mesh: gx: 8 (over y, x, core), sp: 4 (over z).
Axes of the slice: x: 2, y: 2, z: 4, core: 2. Of those that a mesh axis runs over, the one named last changes fastest.
Arguments:
- previous_head: float32 [8, 64, 512], P(None, 'gx', 'sp'), may hold values from -6 to 6
- recharge: float32 [8, 64, 512], P(None, 'gx', 'sp'), may hold values from -6 to 6
- soil_zone: int32 [8, 64, 512], P(None, 'gx', 'sp'), may hold values from 0 to 7
- soil_cond: float32 [8], replicated, may hold values from 0.1 to 1
- soil_store: float32 [8], replicated, may hold values from 0.05 to 0.5
- species: float32 [12, 8, 64, 512], P('sp', None, 'gx'), may hold values from -6 to 6
- mineral_zone: int32 [8, 64, 512], P(None, 'gx', 'sp'), may hold values from 0 to 5
- rate_table: float32 [6, 8], replicated, may hold values from 0.3 to 3
- stoich: float32 [12, 8], replicated, may hold values from -3 to 3
- log_equil: float32 [8], replicated, may hold values from -1 to 1
Outputs:
- head_field: float32 [8, 64, 512], P(None, 'gx', 'sp')
- species_out: float32 [12, 8, 64, 512], P('sp', None, 'gx')
Inputs may be any that keep to these rules, and one draw needn't show every extreme that they name: `soil_zone`: a soil class of 8. `mineral_zone`: a mineral zone class of 6.
All inputs are finite; a program needn't handle non-finite values.
Results may differ from a plain program's by a relative error of at most 0.0003.
Values sent between devices are 32-bit elements; how exact they have to be, the bound alone decides.
No kernel may reach another device: no remote copies, remote signals or barrier semaphores. Data moves between devices by JAX's collectives and lax.ppermute only.
A program may use at most 64 MiB of HBM per device.

v0:
```python
import jax
import jax.numpy as jnp
from jax import lax
from jax.sharding import PartitionSpec as P

ITERS = 6
NEWTON = 2


time_step = 0.05
dispersion = 0.5
reaction_span = 0.5
newton_damping = 0.5


def padded_2(cells, sides, width):
    for axis, dim in sides:
        count = lax.axis_size(axis)
        ends = count - 1
        head = lax.slice_in_dim(cells, 0, width, axis=dim)
        tail = lax.slice_in_dim(cells, cells.shape[dim] - width, cells.shape[dim], axis=dim)
        cells = jnp.concatenate(
            [
                lax.ppermute(tail, axis, [(i, (i + 1) % count) for i in range(ends)]),
                cells,
                lax.ppermute(head, axis, [((i + 1) % count, i) for i in range(ends)]),
            ],
            axis=dim,
        )
    return cells


def harmonic(center, other):
    return 2.0 * center * other / (center + other)


def six_sides(padded):
    return [
        padded[..., 2:, 1:-1, 1:-1],
        padded[..., :-2, 1:-1, 1:-1],
        padded[..., 1:-1, 2:, 1:-1],
        padded[..., 1:-1, :-2, 1:-1],
        padded[..., 1:-1, 1:-1, 2:],
        padded[..., 1:-1, 1:-1, :-2],
    ]


def lookup(labels, entries):
    levels = jnp.arange(entries.shape[0], dtype=jnp.int32).reshape((-1,) + (1,) * labels.ndim)
    return jnp.sum(jnp.where(labels[None] == levels, entries.reshape(levels.shape), 0.0), axis=0)


def lookup_rows(labels, entries):
    levels = jnp.arange(entries.shape[0], dtype=jnp.int32)[:, None, None]
    return jnp.sum(jnp.where(labels[None, None, :] == levels, entries[:, :, None], 0.0), axis=0)


def transport(concentration, conc_padded, head_padded, cond_padded):
    head_center = head_padded[1:-1, 1:-1, 1:-1]
    conduct = cond_padded[1:-1, 1:-1, 1:-1]
    change = jnp.zeros_like(concentration)
    for beside, head_beside, cond_beside in zip(
        six_sides(conc_padded), six_sides(head_padded), six_sides(cond_padded)
    ):
        face_cond = harmonic(conduct, cond_beside)
        velocity = face_cond * (head_center - head_beside)
        change = (
            change
            + jnp.maximum(velocity, 0.0) * concentration
            + jnp.minimum(velocity, 0.0) * beside
        )
        change = change + dispersion * face_cond * (concentration - beside)
    return concentration - time_step * change


def solve_system(jacobian, mismatch):
    dimension = mismatch.shape[0]
    factor = [[None] * dimension for i in range(dimension)]
    inverse = [None] * dimension
    for j in range(dimension):
        for i in range(j, dimension):
            running = jacobian[i * dimension + j] + (1.0 if i == j else 0.0)
            for k in range(j):
                running = running - factor[i][k] * factor[j][k]
            if i == j:
                diag_root = jnp.sqrt(running)
                factor[j][j] = diag_root
                inverse[j] = 1.0 / diag_root
            else:
                factor[i][j] = running * inverse[j]
    forward = []
    for i in range(dimension):
        running = mismatch[i]
        for k in range(i):
            running = running - factor[i][k] * forward[k]
        forward.append(running * inverse[i])
    answer = [None] * dimension
    for i in reversed(range(dimension)):
        running = forward[i]
        for k in range(i + 1, dimension):
            running = running - factor[k][i] * answer[k]
        answer[i] = running * inverse[i]
    return jnp.stack(answer, 0)


def reaction(concentration, labels, rate_table, stoich, log_equil):
    rate_cells = lookup_rows(labels, rate_table)
    pair_products = (stoich[:, None, :] * stoich[None, :, :]).reshape(-1, stoich.shape[1])
    iterate = concentration
    for newton_pass in range(NEWTON):
        affinity = (
            jnp.dot(
                stoich.T,
                iterate,
                precision=lax.Precision.HIGHEST,
                preferred_element_type=jnp.float32,
            )
            - log_equil[:, None]
        )
        tangent = jnp.tanh(affinity)
        mismatch = (
            iterate
            - concentration
            + reaction_span
            * jnp.dot(
                stoich,
                rate_cells * tangent,
                precision=lax.Precision.HIGHEST,
                preferred_element_type=jnp.float32,
            )
        )
        jacobian = reaction_span * jnp.dot(
            pair_products,
            rate_cells * (1.0 - tangent * tangent),
            precision=lax.Precision.HIGHEST,
            preferred_element_type=jnp.float32,
        )
        iterate = iterate - newton_damping * solve_system(jacobian, mismatch)
    return iterate


def pad_vertical(field):
    return jnp.pad(field, ((1, 1), (0, 0), (0, 0)))


def to_cells(block):
    return lax.all_to_all(block, "sp", split_axis=3, concat_axis=0, tiled=True)


def per_device(
    previous_head,
    recharge,
    soil_zone,
    soil_cond,
    soil_store,
    species,
    mineral_zone,
    rate_table,
    stoich,
    log_equil,
):
    conduct = lookup(soil_zone, soil_cond)
    storage = lookup(soil_zone, soil_store)
    cond_padded = pad_vertical(padded_2(conduct, (("gx", 1), ("sp", 2)), 1))
    faces = [harmonic(conduct, beside) for beside in six_sides(cond_padded)]

    def operate(field):
        padded = pad_vertical(padded_2(field, (("gx", 1), ("sp", 2)), 1))
        result = storage * field
        for face_cond, beside in zip(faces, six_sides(padded)):
            result = result + face_cond * (field - beside)
        return result

    source = storage * previous_head + recharge
    head_field = jnp.zeros_like(source)
    residual = source

    def inner_pair(first, second):
        return lax.psum((jnp.sum(first * first), jnp.sum(first * second)), ("gx", "sp"))

    image = operate(residual)
    norm_now, product = inner_pair(residual, image)
    alpha = norm_now / product
    direction = residual
    along = image
    for iteration in range(ITERS):
        head_field = head_field + alpha * direction
        residual = residual - alpha * along
        if iteration + 1 < ITERS:
            image = operate(residual)
            norm_next, product = inner_pair(residual, image)
            ratio = norm_next / norm_now
            alpha = norm_next / (product - ratio * norm_next / alpha)
            direction = residual + ratio * direction
            along = image + ratio * along
            norm_now = norm_next
    head_rows, cond_rows = (
        lax.all_gather(head_field, "sp", axis=2, tiled=True),
        lax.all_gather(conduct, "sp", axis=2, tiled=True),
    )
    stacked = jnp.concatenate([species, head_rows[None], cond_rows[None]], 0)
    padded = padded_2(stacked, (("gx", 2),), 1)
    padded = jnp.pad(padded, ((0, 0), (1, 1), (0, 0), (1, 1)))
    moved = transport(species, padded[:-2], padded[-2], padded[-1])
    cells = to_cells(moved)
    block_shape = cells.shape
    reacted = reaction(
        cells.reshape(block_shape[0], -1), mineral_zone.reshape(-1), rate_table, stoich, log_equil
    )
    reacted = reacted.reshape(block_shape)
    species_out = lax.all_to_all(reacted, "sp", split_axis=0, concat_axis=3, tiled=True)
    return (head_field, species_out)


def solution(mesh):
    in_specs = (
        P(None, "gx", "sp"),
        P(None, "gx", "sp"),
        P(None, "gx", "sp"),
        P(),
        P(),
        P("sp", None, "gx", None),
        P(None, "gx", "sp"),
        P(),
        P(),
        P(),
    )
    out_specs = (P(None, "gx", "sp"), P("sp", None, "gx", None))
    return jax.shard_map(
        per_device, mesh=mesh, in_specs=in_specs, out_specs=out_specs, check_vma=False
    )
```

profile of v0, /device:TPU:0, one launch (start us, length us, event | category | flops | bytes accessed | tf_op | source)
XLA Modules:
  0.0 519.0 jit_solution(3128671705888314182)
XLA Ops:
  6.7 4.5 collective-permute-start.4
  18.8 5.2 collective-permute-start.6
  27.0 43.0 %all-reduce.13 = (f32[]{:T(128)}, f32[]{:T(128)}) all-reduce(f32[]{:T(128)} %get-tuple-element.13, f32[]{:T(128)} %get-tuple-element.12), channel_id=1, replica_groups=mesh['gx'=8,'sp'=4] {'gx','sp'}, use_global_device_ids=true, to_apply=%region_2.3 | all-reduce | flops 2 | bytes 16 | tf_op jit(solution)/shard_map/psum | solution.py:179
  74.0 4.3 collective-permute-done.9
  79.7 4.5 collective-permute-start.10
  87.1 42.6 %all-reduce.12 = (f32[]{:T(128)}, f32[]{:T(128)}) all-reduce(f32[]{:T(128)} %get-tuple-element.11, f32[]{:T(128)} %get-tuple-element.10), channel_id=1, replica_groups=mesh['gx'=8,'sp'=4] {'gx','sp'}, use_global_device_ids=true, to_apply=%region_7.8 | all-reduce | flops 2 | bytes 16 | tf_op jit(solution)/shard_map/psum | solution.py:179
  142.7 4.5 collective-permute-start.14
  150.0 42.4 %all-reduce.11 = (f32[]{:T(128)}, f32[]{:T(128)}) all-reduce(f32[]{:T(128)} %get-tuple-element.9, f32[]{:T(128)} %get-tuple-element.8), channel_id=1, replica_groups=mesh['gx'=8,'sp'=4] {'gx','sp'}, use_global_device_ids=true, to_apply=%region_11.12 | all-reduce | flops 2 | bytes 16 | tf_op jit(solution)/shard_map/psum | solution.py:179
  204.6 4.5 collective-permute-start.18
  212.0 42.3 %all-reduce.10 = (f32[]{:T(128)}, f32[]{:T(128)}) all-reduce(f32[]{:T(128)} %get-tuple-element.7, f32[]{:T(128)} %get-tuple-element.6), channel_id=1, replica_groups=mesh['gx'=8,'sp'=4] {'gx','sp'}, use_global_device_ids=true, to_apply=%region_15.16 | all-reduce | flops 2 | bytes 16 | tf_op jit(solution)/shard_map/psum | solution.py:179
  266.5 4.5 collective-permute-start.22
  273.8 42.4 %all-reduce.9 = (f32[]{:T(128)}, f32[]{:T(128)}) all-reduce(f32[]{:T(128)} %get-tuple-element.5, f32[]{:T(128)} %get-tuple-element.4), channel_id=1, replica_groups=mesh['gx'=8,'sp'=4] {'gx','sp'}, use_global_device_ids=true, to_apply=%region_19.20 | all-reduce | flops 2 | bytes 16 | tf_op jit(solution)/shard_map/psum | solution.py:179
  329.0 4.5 collective-permute-start.26
  333.6 13.7 %all_gather.7 = f32[8,8,512]{2,1,0:T(8,128)S(1)} all-gather(f32[8,8,128]{2,1,0:T(8,128)S(1)} %get-tuple-element.14), channel_id=1, replica_groups=mesh['gx'=8,'sp'=4] {'sp'}, dimensions={2}, use_global_device_ids=true | all-gather | bytes 163840 | tf_op jit(solution)/shard_map/all_gather | solution.py:199
  348.2 39.4 %all-reduce.8 = (f32[]{:T(128)}, f32[]{:T(128)}) all-reduce(f32[]{:T(128)} %get-tuple-element.210, f32[]{:T(128)} %fusion.320), channel_id=1, replica_groups=mesh['gx'=8,'sp'=4] {'gx','sp'}, use_global_device_ids=true, to_apply=%region_23.24 | all-reduce | flops 2 | bytes 16 | tf_op jit(solution)/shard_map/psum | solution.py:179
  391.5 13.5 %all_gather.6 = f32[8,8,512]{2,1,0:T(8,128)S(1)} all-gather(f32[8,8,128]{2,1,0:T(8,128)S(1)} %multiply_add_fusion), channel_id=1, replica_groups=mesh['gx'=8,'sp'=4] {'sp'}, dimensions={2}, use_global_device_ids=true | all-gather | bytes 163840 | tf_op jit(solution)/shard_map/all_gather | solution.py:198
  419.4 6.1 %reshape.95 = f32[4,1,24576]{2,1,0:T(1,128)} reshape(f32[512,3,8,8]{3,2,1,0:T(8,128)} %bitcast.69) | data formatting | bytes 786432
  429.5 10.4 %all-to-all-done = f32[4,1,24576]{2,1,0:T(1,128)S(1)} async-done(((f32[4,1,24576]{2,1,0:T(1,128)}), f32[4,1,24576]{2,1,0:T(1,128)S(1)}, u32[]{:S(2)}, u32[]{:S(2)}) %all-to-all-start) | async-done | bytes 393248 | tf_op jit(solution)/shard_map/all_to_all | solution.py:147
  442.2 6.2 %reshape.96 = f32[512,3,8,8]{3,2,1,0:T(8,128)} reshape(f32[4,24576]{1,0:T(4,128)S(1)} %reduce) | data formatting | bytes 786432
  448.4 4.3 copy.55
  457.8 7.2 %subtract_multiply_fusion.64 = (f32[1,8192]{1,0:T(1,128)S(1)}, f32[1,8192]{1,0:T(1,128)S(1)}, f32[1,8192]{1,0:T(1,128)S(1)}, f32[1,8192]{1,0:T(1,128)S(1)}, f32[...) fusion(f32[12,8192]{1,0:T(8,128)S(1)} %fusion.3, ...), kind=kLoop, calls=%fused_computation.862 | loop fusion | flops 5136384 | bytes 4751360 | tf_op jit(solution)/shard_map/mul | solution.py:96
  465.1 12.1 %subtract_multiply_fusion.57 = (f32[1,8192]{1,0:T(1,128)S(1)}, f32[1,8192]{1,0:T(1,128)S(1)}, f32[1,8192]{1,0:T(1,128)S(1)}, f32[1,8192]{1,0:T(1,128)S(1)}, f32[...) fusion(f32[1,8192]{1,0:T(1,128)S(1)} %get-tuple-element.142, ...), kind=kLoop, calls=%fused_computation.854 | loop fusion | flops 1654784 | bytes 2883584 | tf_op jit(solution)/shard_map/mul | solution.py:90
  487.0 7.3 %subtract_multiply_fusion.18 = (f32[1,8192]{1,0:T(1,128)S(1)}, f32[1,8192]{1,0:T(1,128)S(1)}, f32[1,8192]{1,0:T(1,128)S(1)}, f32[1,8192]{1,0:T(1,128)S(1)}, f32[...) fusion(f32[12,8192]{1,0:T(8,128)S(1)} %fusion.1, ...), kind=kLoop, calls=%fused_computation.808 | loop fusion | flops 5136384 | bytes 4751360 | tf_op jit(solution)/shard_map/mul | solution.py:96
  501.6 16.4 %all_to_all.33 = f32[12,8,8,128]{3,2,1,0:T(8,128)S(1)} all-to-all(f32[12,8,8,128]{3,2,1,0:T(8,128)S(1)} %fusion.11), channel_id=1, replica_groups=mesh['gx'=8,'sp'=4] {'sp'}, dimensions={0} | all-to-all | bytes 786432 | tf_op jit(solution)/shard_map/all_to_all | solution.py:211
  (161 shorter events, 109.5 us)
Async XLA Ops:
  1.5 10.9 %collective-permute-start.1 = (f32[8,1,128]{2,1,0:T(1,128)S(1)}, f32[8,1,128]{2,1,0:T(1,128)S(1)}, u32[]{:S(2)}, u32[]{:S(2)}) collective-permute-start(f32[8,1,128]{2,1,0:T(1,128)S(1)} %get-tuple-element.269), channel_id=1, source_target_pairs={{4,0},{8,4},{12,8},{16,12},{20,16},{24,20},{28,24},{5,1},{9,5},{13... | collective-permute-start | bytes 12296 | tf_op jit(solution)/shard_map/ppermute | solution.py:26
  2.8 9.6 %collective-permute-start = (f32[8,1,128]{2,1,0:T(1,128)S(1)}, f32[8,1,128]{2,1,0:T(1,128)S(1)}, u32[]{:S(2)}, u32[]{:S(2)}) collective-permute-start(f32[8,1,128]{2,1,0:T(1,128)S(1)} %get-tuple-element.270), channel_id=1, source_target_pairs={{0,4},{4,8},{8,12},{12,16},{16,20},{20,24},{24,28},{1,5},{5,9},{9,... | collective-permute-start | bytes 12296 | tf_op jit(solution)/shard_map/ppermute | solution.py:24
  6.7 10.7 %collective-permute-start.4 = (f32[8,1,128]{2,1,0:T(1,128)S(1)}, f32[8,1,128]{2,1,0:T(1,128)S(1)}, u32[]{:S(2)}, u32[]{:S(2)}) collective-permute-start(f32[8,1,128]{2,1,0:T(1,128)S(1)} %get-tuple-element.271), channel_id=1, source_target_pairs={{0,4},{4,8},{8,12},{12,16},{16,20},{20,24},{24,28},{1,5},{5,9},{9,... | collective-permute-start | bytes 12296 | tf_op jit(solution)/shard_map/ppermute | solution.py:24
  11.2 6.2 %collective-permute-start.5 = (f32[8,1,128]{2,1,0:T(1,128)S(1)}, f32[8,1,128]{2,1,0:T(1,128)S(1)}, u32[]{:S(2)}, u32[]{:S(2)}) collective-permute-start(f32[8,1,128]{2,1,0:T(1,128)S(1)} %get-tuple-element.272), channel_id=1, source_target_pairs={{4,0},{8,4},{12,8},{16,12},{20,16},{24,20},{28,24},{5,1},{9,5},{13... | collective-permute-start | bytes 12296 | tf_op jit(solution)/shard_map/ppermute | solution.py:26
  12.6 11.4 %collective-permute-start.2 = (f32[8,10,1]{2,1,0:T(8,128)S(1)}, f32[8,10,1]{2,1,0:T(8,128)S(1)}, u32[]{:S(2)}, u32[]{:S(2)}) collective-permute-start(f32[8,10,1]{2,1,0:T(8,128)S(1)} %get-tuple-element.255), channel_id=1, source_target_pairs={{0,1},{1,2},{2,3},{4,5},{5,6},{6,7},{8,9},{9,10},{10,11},{12,13},{... | collective-permute-start | bytes 968 | tf_op jit(solution)/shard_map/ppermute | solution.py:24
  16.1 7.9 %collective-permute-start.3 = (f32[8,10,1]{2,1,0:T(8,128)S(1)}, f32[8,10,1]{2,1,0:T(8,128)S(1)}, u32[]{:S(2)}, u32[]{:S(2)}) collective-permute-start(f32[8,10,1]{2,1,0:T(8,128)S(1)} %get-tuple-element.256), channel_id=1, source_target_pairs={{1,0},{2,1},{3,2},{5,4},{6,5},{7,6},{9,8},{10,9},{11,10},{13,12},{... | collective-permute-start | bytes 968 | tf_op jit(solution)/shard_map/ppermute | solution.py:26
  17.5 7.4 %collective-permute-start.7 = (f32[8,10,1]{2,1,0:T(8,128)S(1)}, f32[8,10,1]{2,1,0:T(8,128)S(1)}, u32[]{:S(2)}, u32[]{:S(2)}) collective-permute-start(f32[8,10,1]{2,1,0:T(8,128)S(1)} %get-tuple-element.257), channel_id=1, source_target_pairs={{1,0},{2,1},{3,2},{5,4},{6,5},{7,6},{9,8},{10,9},{11,10},{13,12},{... | collective-permute-start | bytes 968 | tf_op jit(solution)/shard_map/ppermute | solution.py:26
  18.8 7.3 %collective-permute-start.6 = (f32[8,10,1]{2,1,0:T(8,128)S(1)}, f32[8,10,1]{2,1,0:T(8,128)S(1)}, u32[]{:S(2)}, u32[]{:S(2)}) collective-permute-start(f32[8,10,1]{2,1,0:T(8,128)S(1)} %get-tuple-element.258), channel_id=1, source_target_pairs={{0,1},{1,2},{2,3},{4,5},{5,6},{6,7},{8,9},{9,10},{10,11},{12,13},{... | collective-permute-start | bytes 968 | tf_op jit(solution)/shard_map/ppermute | solution.py:24
  72.7 5.6 %collective-permute-start.9 = (f32[8,1,128]{2,1,0:T(1,128)S(1)}, f32[8,1,128]{2,1,0:T(1,128)S(1)}, u32[]{:S(2)}, u32[]{:S(2)}) collective-permute-start(f32[8,1,128]{2,1,0:T(1,128)S(1)} %get-tuple-element.268), channel_id=1, source_target_pairs={{4,0},{8,4},{12,8},{16,12},{20,16},{24,20},{28,24},{5,1},{9,5},{13... | collective-permute-start | bytes 12296 | tf_op jit(solution)/shard_map/ppermute | solution.py:26
  78.4 6.2 %collective-permute-start.11 = (f32[8,10,1]{2,1,0:T(8,128)S(1)}, f32[8,10,1]{2,1,0:T(8,128)S(1)}, u32[]{:S(2)}, u32[]{:S(2)}) collective-permute-start(f32[8,10,1]{2,1,0:T(8,128)S(1)} %get-tuple-element.253), channel_id=1, source_target_pairs={{1,0},{2,1},{3,2},{5,4},{6,5},{7,6},{9,8},{10,9},{11,10},{13,12},{... | collective-permute-start | bytes 968 | tf_op jit(solution)/shard_map/ppermute | solution.py:26
  79.7 6.4 %collective-permute-start.10 = (f32[8,10,1]{2,1,0:T(8,128)S(1)}, f32[8,10,1]{2,1,0:T(8,128)S(1)}, u32[]{:S(2)}, u32[]{:S(2)}) collective-permute-start(f32[8,10,1]{2,1,0:T(8,128)S(1)} %get-tuple-element.254), channel_id=1, source_target_pairs={{0,1},{1,2},{2,3},{4,5},{5,6},{6,7},{8,9},{9,10},{10,11},{12,13},{... | collective-permute-start | bytes 968 | tf_op jit(solution)/shard_map/ppermute | solution.py:24
  135.6 5.6 %collective-permute-start.13 = (f32[8,1,128]{2,1,0:T(1,128)S(1)}, f32[8,1,128]{2,1,0:T(1,128)S(1)}, u32[]{:S(2)}, u32[]{:S(2)}) collective-permute-start(f32[8,1,128]{2,1,0:T(1,128)S(1)} %get-tuple-element.266), channel_id=1, source_target_pairs={{4,0},{8,4},{12,8},{16,12},{20,16},{24,20},{28,24},{5,1},{9,5},{13... | collective-permute-start | bytes 12296 | tf_op jit(solution)/shard_map/ppermute | solution.py:26
  141.2 6.3 %collective-permute-start.15 = (f32[8,10,1]{2,1,0:T(8,128)S(1)}, f32[8,10,1]{2,1,0:T(8,128)S(1)}, u32[]{:S(2)}, u32[]{:S(2)}) collective-permute-start(f32[8,10,1]{2,1,0:T(8,128)S(1)} %get-tuple-element.251), channel_id=1, source_target_pairs={{1,0},{2,1},{3,2},{5,4},{6,5},{7,6},{9,8},{10,9},{11,10},{13,12},{... | collective-permute-start | bytes 968 | tf_op jit(solution)/shard_map/ppermute | solution.py:26
  142.7 6.4 %collective-permute-start.14 = (f32[8,10,1]{2,1,0:T(8,128)S(1)}, f32[8,10,1]{2,1,0:T(8,128)S(1)}, u32[]{:S(2)}, u32[]{:S(2)}) collective-permute-start(f32[8,10,1]{2,1,0:T(8,128)S(1)} %get-tuple-element.252), channel_id=1, source_target_pairs={{0,1},{1,2},{2,3},{4,5},{5,6},{6,7},{8,9},{9,10},{10,11},{12,13},{... | collective-permute-start | bytes 968 | tf_op jit(solution)/shard_map/ppermute | solution.py:24
  197.7 5.6 %collective-permute-start.17 = (f32[8,1,128]{2,1,0:T(1,128)S(1)}, f32[8,1,128]{2,1,0:T(1,128)S(1)}, u32[]{:S(2)}, u32[]{:S(2)}) collective-permute-start(f32[8,1,128]{2,1,0:T(1,128)S(1)} %get-tuple-element.264), channel_id=1, source_target_pairs={{4,0},{8,4},{12,8},{16,12},{20,16},{24,20},{28,24},{5,1},{9,5},{13... | collective-permute-start | bytes 12296 | tf_op jit(solution)/shard_map/ppermute | solution.py:26
  203.3 6.2 %collective-permute-start.19 = (f32[8,10,1]{2,1,0:T(8,128)S(1)}, f32[8,10,1]{2,1,0:T(8,128)S(1)}, u32[]{:S(2)}, u32[]{:S(2)}) collective-permute-start(f32[8,10,1]{2,1,0:T(8,128)S(1)} %get-tuple-element.249), channel_id=1, source_target_pairs={{1,0},{2,1},{3,2},{5,4},{6,5},{7,6},{9,8},{10,9},{11,10},{13,12},{... | collective-permute-start | bytes 968 | tf_op jit(solution)/shard_map/ppermute | solution.py:26
  204.6 6.4 %collective-permute-start.18 = (f32[8,10,1]{2,1,0:T(8,128)S(1)}, f32[8,10,1]{2,1,0:T(8,128)S(1)}, u32[]{:S(2)}, u32[]{:S(2)}) collective-permute-start(f32[8,10,1]{2,1,0:T(8,128)S(1)} %get-tuple-element.250), channel_id=1, source_target_pairs={{0,1},{1,2},{2,3},{4,5},{5,6},{6,7},{8,9},{9,10},{10,11},{12,13},{... | collective-permute-start | bytes 968 | tf_op jit(solution)/shard_map/ppermute | solution.py:24
  265.2 6.2 %collective-permute-start.23 = (f32[8,10,1]{2,1,0:T(8,128)S(1)}, f32[8,10,1]{2,1,0:T(8,128)S(1)}, u32[]{:S(2)}, u32[]{:S(2)}) collective-permute-start(f32[8,10,1]{2,1,0:T(8,128)S(1)} %get-tuple-element.247), channel_id=1, source_target_pairs={{1,0},{2,1},{3,2},{5,4},{6,5},{7,6},{9,8},{10,9},{11,10},{13,12},{... | collective-permute-start | bytes 968 | tf_op jit(solution)/shard_map/ppermute | solution.py:26
  266.5 6.4 %collective-permute-start.22 = (f32[8,10,1]{2,1,0:T(8,128)S(1)}, f32[8,10,1]{2,1,0:T(8,128)S(1)}, u32[]{:S(2)}, u32[]{:S(2)}) collective-permute-start(f32[8,10,1]{2,1,0:T(8,128)S(1)} %get-tuple-element.248), channel_id=1, source_target_pairs={{0,1},{1,2},{2,3},{4,5},{5,6},{6,7},{8,9},{9,10},{10,11},{12,13},{... | collective-permute-start | bytes 968 | tf_op jit(solution)/shard_map/ppermute | solution.py:24
  322.1 5.6 %collective-permute-start.25 = (f32[8,1,128]{2,1,0:T(1,128)S(1)}, f32[8,1,128]{2,1,0:T(1,128)S(1)}, u32[]{:S(2)}, u32[]{:S(2)}) collective-permute-start(f32[8,1,128]{2,1,0:T(1,128)S(1)} %get-tuple-element.260), channel_id=1, source_target_pairs={{4,0},{8,4},{12,8},{16,12},{20,16},{24,20},{28,24},{5,1},{9,5},{13... | collective-permute-start | bytes 12296 | tf_op jit(solution)/shard_map/ppermute | solution.py:26
  327.7 19.5 %collective-permute-start.27 = (f32[8,10,1]{2,1,0:T(8,128)S(1)}, f32[8,10,1]{2,1,0:T(8,128)S(1)}, u32[]{:S(2)}, u32[]{:S(2)}) collective-permute-start(f32[8,10,1]{2,1,0:T(8,128)S(1)} %get-tuple-element.245), channel_id=1, source_target_pairs={{1,0},{2,1},{3,2},{5,4},{6,5},{7,6},{9,8},{10,9},{11,10},{13,12},{... | collective-permute-start | bytes 968 | tf_op jit(solution)/shard_map/ppermute | solution.py:26
  329.0 18.2 %collective-permute-start.26 = (f32[8,10,1]{2,1,0:T(8,128)S(1)}, f32[8,10,1]{2,1,0:T(8,128)S(1)}, u32[]{:S(2)}, u32[]{:S(2)}) collective-permute-start(f32[8,10,1]{2,1,0:T(8,128)S(1)} %get-tuple-element.246), channel_id=1, source_target_pairs={{0,1},{1,2},{2,3},{4,5},{5,6},{6,7},{8,9},{9,10},{10,11},{12,13},{... | collective-permute-start | bytes 968 | tf_op jit(solution)/shard_map/ppermute | solution.py:24
  406.5 5.7 %collective-permute-start.29 = (f32[5,8,1,512]{3,1,2,0:T(8,128)S(1)}, f32[5,8,1,512]{3,1,2,0:T(8,128)S(1)}, u32[]{:S(2)}, u32[]{:S(2)}) collective-permute-start(f32[5,8,1,512]{3,1,2,0:T(8,128)S(1)} %get-tuple-element.238), channel_id=1, source_target_pairs={{4,0},{8,4},{12,8},{16,12},{20,16},{24,20},{28,24},{5,1},{9,5},{13... | collective-permute-start | bytes 245768 | tf_op jit(solution)/shard_map/ppermute | solution.py:26
  425.5 14.4 %all-to-all-start = ((f32[4,1,24576]{2,1,0:T(1,128)}), f32[4,1,24576]{2,1,0:T(1,128)S(1)}, u32[]{:S(2)}, u32[]{:S(2)}) async-start(f32[4,1,24576]{2,1,0:T(1,128)} %reshape.95), calls=%async_computation | async-start | bytes 786432 | tf_op jit(solution)/shard_map/all_to_all | solution.py:147
  (13 other events, 258.7 us)
where the time goes:
time: 528 us; the launch traced here: 519 us
  blocking collectives  296 us (56%)
  starting transfers between devices  69.9 us (13%)
  other arithmetic  50.9 us (10%)
  waiting for transfers between devices  45.1 us (9%)
  local copies, waits for them, and re-layouts  24 us (5%)
  between operations  23.3 us (4%)
  matrix products  10.1 us (2%)
    psum x6, blocking collectives, inner_pair(): lax.psum((jnp.sum(first * first), jnp.sum(first * second)), ('gx', 'sp'))  252 us
    ppermute x15, starting transfers between devices, padded_2(): lax.ppermute(tail, axis, [(i, (i + 1) % count) for i in range(ends)])  46.7 us
    ppermute x15, waiting for transfers between devices, padded_2(): lax.ppermute(head, axis, [((i + 1) % count, i) for i in range(ends)])  27.1 us
    ppermute x15, starting transfers between devices, padded_2(): lax.ppermute(head, axis, [((i + 1) % count, i) for i in range(ends)])  19.7 us
    all_to_all x1, blocking collectives, per_device(): lax.all_to_all(reacted, 'sp', split_axis=0, concat_axis=3, tiled=True)  16.4 us
    mul x2, other arithmetic, solve_system(): factor[i][j] = running * inverse[j]  14.8 us
    mul x2, other arithmetic, solve_system(): forward.append(running * inverse[i])  14.5 us
    all_gather x1, blocking collectives, per_device(): lax.all_gather(conduct, 'sp', axis=2, tiled=True)  13.7 us
  transfers between devices with their start and end apart: 31, of which 17 were waited for; matrix products, arithmetic and copies ran while one was open for 0% of the time, Pallas kernels for 0%

commit v1 on v0

v1 whole, which is shorter than its diff:
```python
import functools

import jax
import jax.numpy as jnp
from jax import lax
from jax.experimental import pallas as pl
from jax.experimental.pallas import tpu as pltpu
from jax.sharding import PartitionSpec as P

ITERS = 6
NEWTON = 2

time_step = 0.05
dispersion = 0.5
reaction_span = 0.5
newton_damping = 0.5

LANES = 128
BASIS = ITERS + 1
PAIRS = [(i, j) for j in range(BASIS) for i in range(j + 1)]
PAIR_AT = {pair: at for at, pair in enumerate(PAIRS)}
PAIR_ROWS = -(-len(PAIRS) // 8) * 8


def harmonic(center, other):
    return 2.0 * center * other / jnp.maximum(center + other, 1e-30)


def pick(labels, table, first):
    value = jnp.zeros(labels.shape, jnp.float32)
    for level in range(table.shape[0]):
        value = jnp.where(labels == level + first, table[level], value)
    return value


def lane_ids(shape):
    return lax.broadcasted_iota(jnp.int32, shape, len(shape) - 1)


def pack_kernel(cond_t, store_t, previous, recharge, zone, species, *outs):
    *blocks, stats = outs
    count = len(blocks)
    me = lax.axis_index("sp")
    groups, layers = species.shape[0], species.shape[1]
    shape = previous.shape[1:]
    lane = lane_ids(shape)
    conduct, store_sum, face_sum = [], jnp.zeros(shape), jnp.zeros(shape)
    for z in range(layers):
        labels = zone[z]
        conduct.append(pick(labels, cond_t, 0))
        storage = pick(labels, store_t, 0)
        store_sum = store_sum + storage
        source = storage * previous[z] + recharge[z]
        label = (labels + 1).astype(jnp.float32)
        for d in {1, count - 1}:
            blocks[d][z] = source
            blocks[d][layers + z] = label
    for z in range(layers):
        face_sum = face_sum + 8.0 * harmonic(conduct[z], pltpu.roll(conduct[z], 1, 0))
        if z + 1 < layers:
            face_sum = face_sum + 4.0 * harmonic(conduct[z], conduct[z + 1])
    column = jnp.sum(store_sum + face_sum, axis=0, keepdims=True) * (1.0 / (layers * shape[0]))
    stats[...] = jnp.broadcast_to(jnp.max(column, axis=1, keepdims=True), stats.shape)

    for d in range(count):
        base = blocks[d].shape[0] - groups * layers - 1
        here = lax.rem(me + d, count)
        left = lax.rem(here + count - 1, count)
        right = lax.rem(here + 1, count)
        at = [pl.ds(pl.multiple_of(i * LANES, LANES), LANES) for i in (left, here, right)]
        edge = jnp.zeros(shape, jnp.float32)
        for c in range(groups):
            for z in range(layers):
                j = c * layers + z
                blocks[d][base + j] = species[c, z, :, at[1]]
                edge = jnp.where(lane == 2 * j, pltpu.roll(species[c, z, :, at[2]], 2 * j, 1), edge)
                edge = jnp.where(
                    lane == 2 * j + 1, pltpu.roll(species[c, z, :, at[0]], 2 * j + 2, 1), edge
                )
        blocks[d][base + groups * layers] = edge


def widen_kernel(groups, own_field, *refs):
    *blocks, up, down = refs
    count = len(blocks)
    me = lax.axis_index("sp")
    layers = (blocks[1].shape[0] - blocks[0].shape[0]) // 2
    rows = own_field.shape[1]
    has_left = (me > 0).astype(jnp.float32)
    has_right = (me < count - 1).astype(jnp.float32)
    lane = lane_ids(own_field.shape[1:])
    for t in range(2 * layers):
        near = jnp.where(lane < LANES // 2, blocks[count - 1][t] * has_right, blocks[1][t] * has_left)
        for out in (up, down):
            out[t] = own_field[t]
            out[2 * layers + t] = near
    for d in range(count):
        base = blocks[d].shape[0] - groups * layers - 1
        for c in range(groups):
            at = 4 * layers + d * groups + c
            span = pl.ds(base + c * layers, layers)
            up[at] = blocks[d][span, 0, :]
            down[at] = blocks[d][span, rows - 1, :]


def krylov_kernel(cond_t, store_t, stats, own, above, below, basis, kx, ky, kz, sums, cond_s, store_s, pair_s):
    count = lax.axis_size("gx")
    me = lax.axis_index("gx")
    layers, tall, wide = cond_s.shape
    rows = tall // 3
    keep = ((me > 0).astype(jnp.float32), 1.0, (me < count - 1).astype(jnp.float32))
    top = jnp.max(stats[...], axis=0, keepdims=True)
    top = jnp.concatenate([top] * (wide // LANES), axis=1)
    twice, fourth = 2.0 / top, 4.0 / top

    for z in range(layers):
        for part, (block, use) in enumerate(zip((above, own, below), keep)):
            at = slice(part * rows, (part + 1) * rows)
            for half in range(2):
                cols = slice(half * LANES, (half + 1) * LANES)
                field = block[2 * layers * half + z]
                labels = block[2 * layers * half + layers + z]
                if part != 1:
                    field, labels = field * use, labels * use
                basis[0, z, at, cols] = field
                cond_s[z, at, cols] = pick(labels, cond_t, 1)
                store_s[z, at, cols] = pick(labels, store_t, 1)
    kz[0] = jnp.zeros((tall, wide), jnp.float32)
    for z in range(layers):
        here = cond_s[z]
        kx[z] = harmonic(here, pltpu.roll(here, tall - 1, 0))
        ky[z] = harmonic(here, pltpu.roll(here, wide - 1, 1))
        if z + 1 < layers:
            kz[z + 1] = harmonic(here, cond_s[z + 1])

    def operate(k):
        flow = None
        result = []
        for z in range(layers):
            value = basis[k, z]
            along_x = kx[z] * (value - pltpu.roll(value, tall - 1, 0))
            along_y = ky[z] * (value - pltpu.roll(value, wide - 1, 1))
            image = store_s[z] * value
            image = image + (along_x - pltpu.roll(along_x, 1, 0))
            image = image + (along_y - pltpu.roll(along_y, 1, 1))
            if z + 1 < layers:
                along_z = kz[z + 1] * (value - basis[k, z + 1])
                image = image + along_z
            if z:
                image = image - flow
            flow = along_z
            yield z, value, image

    for z, value, image in operate(0):
        basis[1, z] = image * twice - value

    def step(k, carry):
        for z, value, image in operate(k):
            basis[k + 1, z] = image * fourth - 2.0 * value - basis[k - 1, z]
        return carry

    lax.fori_loop(1, ITERS, step, 0)

    totals = [None] * len(PAIRS)
    for z in range(layers):
        values = [basis[k, z, rows : 2 * rows, :LANES] for k in range(BASIS)]
        for at, (i, j) in enumerate(PAIRS):
            term = values[i] * values[j]
            totals[at] = term if z == 0 else totals[at] + term
    pair_s[...] = jnp.zeros(pair_s.shape, jnp.float32)
    for at, total in enumerate(totals):
        pair_s[at : at + 1, :] = jnp.sum(total, axis=0, keepdims=True)
    full = jnp.sum(pair_s[...], axis=1, keepdims=True)
    lane = lane_ids(pair_s.shape)
    row = lax.broadcasted_iota(jnp.int32, pair_s.shape, 0)
    line = jnp.sum(jnp.where(lane == row, full, 0.0), axis=0, keepdims=True)
    sums[...] = jnp.broadcast_to(line, sums.shape)


def direction_weights(gram, cap):
    def inner(i, j):
        return gram[PAIR_AT[(min(i, j), max(i, j))]]

    def image_inner(i, j):
        if j == 0:
            return 2.0 * (inner(i, 0) + inner(i, 1))
        return inner(i, j + 1) + inner(i, j - 1) + 2.0 * inner(i, j)

    def quadratic(values, form):
        total = None
        for i, left in enumerate(values):
            part = form(i, i) * left
            for j in range(i):
                part = part + 2.0 * form(i, j) * values[j]
            total = left * part if total is None else total + left * part
        return total

    images = {(i, j): image_inner(i, j) for i in range(ITERS) for j in range(i + 1)}
    start = inner(0, 0)
    one = jnp.ones_like(start)
    zero = jnp.zeros_like(start)
    head, residual, direction = [zero] * ITERS, [one], [one]
    norm_now = start
    live = norm_now > 0.0
    for iteration in range(ITERS):
        product = quadratic(direction, lambda i, j: images[(i, j)])
        live = jnp.logical_and(live, product > 0.0)
        alpha = jnp.where(live, jnp.minimum(norm_now / jnp.where(live, product, one), cap), zero)
        for i, part in enumerate(direction):
            head[i] = head[i] + alpha * part
        if iteration + 1 == ITERS:
            return head
        applied = [zero] * (iteration + 2)
        for j, part in enumerate(direction):
            applied[j] = applied[j] + 2.0 * part
            applied[j + 1] = applied[j + 1] + (2.0 * part if j == 0 else part)
            if j:
                applied[j - 1] = applied[j - 1] + part
        residual = residual + [zero]
        residual = [part - alpha * moved for part, moved in zip(residual, applied)]
        norm_next = jnp.maximum(quadratic(residual, inner), 0.0)
        ratio = norm_next / jnp.where(live, norm_now, one)
        live = jnp.logical_and(live, norm_next > 1e-7 * start)
        direction = [part + ratio * past for part, past in zip(residual, direction + [zero])]
        norm_now = norm_next


def react(moved, rates, powers, stoich, rows, log_equil):
    minerals = len(rates)
    first = []
    for m in range(minerals):
        total = None
        for value, row in zip(moved, rows):
            term = stoich[row, m] * value
            total = term if total is None else total + term
        first.append(total - log_equil[m])
    shift = None
    for newton_pass in range(NEWTON):
        if shift is None:
            affinity = first
        else:
            affinity = []
            for m in range(minerals):
                total = first[m]
                for n in range(minerals):
                    total = total - powers[m, n] * shift[n]
                affinity.append(total)
        tangent = [jnp.tanh(value) for value in affinity]
        gap = [reaction_span * rate * value for rate, value in zip(rates, tangent)]
        if shift is not None:
            gap = [value - past for value, past in zip(gap, shift)]
        root = [jnp.sqrt(reaction_span * rate * (1.0 - value * value)) for rate, value in zip(rates, tangent)]
        matrix = {}
        for i in range(minerals):
            for j in range(i + 1):
                entry = root[i] * root[j] * powers[i, j]
                matrix[(i, j)] = entry + 1.0 if i == j else entry
        right = []
        for i in range(minerals):
            total = None
            for j in range(minerals):
                term = powers[i, j] * gap[j]
                total = term if total is None else total + term
            right.append(root[i] * total)
        inverse = [None] * minerals
        for j in range(minerals):
            inverse[j] = lax.rsqrt(matrix[(j, j)])
            for i in range(j + 1, minerals):
                matrix[(i, j)] = matrix[(i, j)] * inverse[j]
            right[j] = right[j] * inverse[j]
            for i in range(j + 1, minerals):
                right[i] = right[i] - matrix[(i, j)] * right[j]
                for k in range(j + 1, i + 1):
                    matrix[(i, k)] = matrix[(i, k)] - matrix[(i, j)] * matrix[(k, j)]
        for i in reversed(range(minerals)):
            right[i] = right[i] * inverse[i]
            for k in range(i):
                right[k] = right[k] - matrix[(i, k)] * right[i]
        delta = [newton_damping * (g - e * w) for g, e, w in zip(gap, root, right)]
        shift = delta if shift is None else [past + step for past, step in zip(shift, delta)]
    result = []
    for value, row in zip(moved, rows):
        for m in range(minerals):
            value = value - stoich[row, m] * shift[m]
        result.append(value)
    return result


def finish_kernel(groups, store_t, rate_t, stoich, powers, log_equil, stats, sums, mineral, basis, kx, ky, kz, above, below, *refs):
    count = lax.axis_size("sp")
    blocks, (head_out, *outs) = refs[:count], refs[count : 2 * count + 1]
    head_s, pair_s = refs[2 * count + 1 :]
    me = lax.axis_index("sp")
    layers, rows = head_out.shape[:2]
    tall, wide = head_s.shape[1:]

    total = jnp.sum(sums[...], axis=0, keepdims=True)
    lane = lane_ids(pair_s.shape)
    row = lax.broadcasted_iota(jnp.int32, pair_s.shape, 0)
    spread = jnp.sum(jnp.where(lane == row, total, 0.0), axis=1, keepdims=True)
    pair_s[...] = jnp.broadcast_to(spread, pair_s.shape)
    top = jnp.max(stats[...], axis=0, keepdims=True)
    low = store_t[0]
    for k in range(1, store_t.shape[0]):
        low = jnp.minimum(low, store_t[k])
    gram = [pair_s[at : at + 1, :] for at in range(len(PAIRS))]
    weights = direction_weights(gram, top / (4.0 * low))
    weights = [jnp.concatenate([w * (4.0 / top)] * (wide // LANES), axis=1) for w in weights]
    for z in range(layers):
        value = weights[0] * basis[0, z]
        for k in range(1, ITERS):
            value = value + weights[k] * basis[k, z]
        head_s[z] = value
        head_out[z] = value[rows : 2 * rows, :LANES]

    shape = (rows, LANES)
    lane = lane_ids(shape)
    row = lax.broadcasted_iota(jnp.int32, shape, 0)
    center = slice(rows, 2 * rows)

    def layer(z, carry):
        before, after = jnp.maximum(z - 1, 0), jnp.minimum(z + 1, layers - 1)
        value = head_s[z, :, :LANES]
        face = kx[z, :, :LANES]
        flow = face * (value - pltpu.roll(value, tall - 1, 0))
        faces = [(face[center], flow[center])]
        faces.append((pltpu.roll(face, 1, 0)[center], -pltpu.roll(flow, 1, 0)[center]))
        value = head_s[z, center, :]
        face = ky[z, center, :]
        flow = face * (value - pltpu.roll(value, wide - 1, 1))
        faces.append((face[:, :LANES], flow[:, :LANES]))
        faces.append((pltpu.roll(face, 1, 1)[:, :LANES], -pltpu.roll(flow, 1, 1)[:, :LANES]))
        value = value[:, :LANES]
        for face, other in ((kz[z + 1, center, :LANES], after), (kz[z, center, :LANES], before)):
            faces.append((face, face * (value - head_s[other, center, :LANES])))
        outward = None
        inward = []
        for face, flow in faces:
            term = jnp.maximum(flow, 0.0) + dispersion * face
            outward = term if outward is None else outward + term
            inward.append(time_step * (dispersion * face - jnp.minimum(flow, 0.0)))
        stay = 1.0 - time_step * outward

        moved, table_rows = [], []
        for d, block in enumerate(blocks):
            base = block.shape[0] - groups * layers - 1
            group = lax.rem(me + count - d, count)
            edge = block[base + groups * layers]
            for c in range(groups):
                at = base + c * layers
                here = block[at + z]
                side = pltpu.roll(edge, LANES - 1 - 2 * (c * layers + z), 1)
                line = pl.ds(z, 1)
                edge_at = 4 * layers + d * groups + c
                following = jnp.where(row == rows - 1, below[edge_at, line, :], pltpu.roll(here, rows - 1, 0))
                preceding = jnp.where(row == 0, above[edge_at, line, :], pltpu.roll(here, 1, 0))
                result = stay * here + inward[0] * following + inward[1] * preceding
                result = result + inward[2] * jnp.where(lane == LANES - 1, side, pltpu.roll(here, LANES - 1, 1))
                result = result + inward[3] * jnp.where(lane == 0, side, pltpu.roll(here, 1, 1))
                result = result + inward[4] * block[at + after] + inward[5] * block[at + before]
                moved.append(result)
                table_rows.append(group * groups + c)
        labels = mineral[z]
        rates = []
        for m in range(rate_t.shape[1]):
            rate = jnp.zeros(shape, jnp.float32)
            for level in range(rate_t.shape[0]):
                rate = jnp.where(labels == level, rate_t[level, m], rate)
            rates.append(rate)
        reacted = react(moved, rates, powers, stoich, table_rows, log_equil)
        for at, result in enumerate(reacted):
            outs[at // groups][(at % groups) * layers + z] = result
        return carry

    lax.fori_loop(0, layers, layer, 0)


def place_kernel(*refs):
    *blocks, out = refs
    count = len(blocks)
    me = lax.axis_index("sp")
    groups, layers = out.shape[:2]
    for d, block in enumerate(blocks):
        column = pl.multiple_of(lax.rem(me + d, count) * LANES, LANES)
        for c in range(groups):
            for z in range(layers):
                out[c, z, :, pl.ds(column, LANES)] = block[c * layers + z]


def call(kernel, tables, arrays, out_shapes, scratch=()):
    smem = pl.BlockSpec(memory_space=pltpu.SMEM)
    vmem = pl.BlockSpec(memory_space=pltpu.VMEM)
    shapes = [jax.ShapeDtypeStruct(shape, jnp.float32) for shape in out_shapes]
    return pl.pallas_call(
        kernel,
        out_shape=shapes,
        in_specs=[smem] * len(tables) + [vmem] * len(arrays),
        out_specs=[vmem] * len(shapes),
        scratch_shapes=[pltpu.VMEM(shape, jnp.float32) for shape in scratch],
    )(*tables, *arrays)


def shifted(array, axis, amount):
    count = lax.axis_size(axis)
    return lax.ppermute(array, axis, [(i, (i + amount) % count) for i in range(count)])


def per_device(
    previous_head,
    recharge,
    soil_zone,
    soil_cond,
    soil_store,
    species,
    mineral_zone,
    rate_table,
    stoich,
    log_equil,
):
    count = lax.axis_size("sp")
    devices = count * lax.axis_size("gx")
    layers, rows, columns = previous_head.shape
    groups = species.shape[0]
    assert columns == LANES and layers == 8 and rows == 8 and count > 2
    own_tiles = groups * layers + 1
    tile = (rows, LANES)

    tiles = [own_tiles + (2 * layers if d in (1, count - 1) else 0) for d in range(count)]
    *blocks, stats = call(
        pack_kernel,
        [soil_cond, soil_store],
        [previous_head, recharge, soil_zone, species],
        [(t,) + tile for t in tiles] + [(devices, LANES)],
    )
    field = blocks[1]
    blocks = [blocks[0]] + [shifted(blocks[d], "sp", d) for d in range(1, count)]
    stats = lax.all_to_all(stats, ("gx", "sp"), 0, 0, tiled=True)
    wide_tiles = 4 * layers + count * groups
    up, down = call(
        functools.partial(widen_kernel, groups), [], [field] + blocks, [(wide_tiles,) + tile] * 2
    )
    below, above = shifted(up, "gx", -1), shifted(down, "gx", 1)
    extended = (layers, 3 * rows, 2 * LANES)
    basis, kx, ky, kz, sums = call(
        krylov_kernel,
        [soil_cond, soil_store],
        [stats, up, above, below],
        [(BASIS,) + extended, extended, extended, (layers + 1,) + extended[1:], (devices, LANES)],
        [extended, extended, (PAIR_ROWS, LANES)],
    )
    sums = lax.all_to_all(sums, ("gx", "sp"), 0, 0, tiled=True)
    powers = jnp.dot(stoich.T, stoich, precision=lax.Precision.HIGHEST, preferred_element_type=jnp.float32)
    head_field, *reacted = call(
        functools.partial(finish_kernel, groups),
        [soil_store, rate_table, stoich, powers, log_equil],
        [stats, sums, mineral_zone, basis, kx, ky, kz, above, below] + blocks,
        [(layers,) + tile] + [(groups * layers,) + tile] * count,
        [extended, (PAIR_ROWS, LANES)],
    )
    reacted = [reacted[0]] + [shifted(reacted[d], "sp", -d) for d in range(1, count)]
    (species_out,) = call(place_kernel, [], reacted, [species.shape])
    return (head_field, species_out)


def solution(mesh):
    in_specs = (
        P(None, "gx", "sp"),
        P(None, "gx", "sp"),
        P(None, "gx", "sp"),
        P(),
        P(),
        P("sp", None, "gx", None),
        P(None, "gx", "sp"),
        P(),
        P(),
        P(),
    )
    out_specs = (P(None, "gx", "sp"), P("sp", None, "gx", None))
    return jax.shard_map(
        per_device, mesh=mesh, in_specs=in_specs, out_specs=out_specs, check_vma=False
    )
```

time: 528 us -> 72.2 us (0.14); the launches traced: 519 us -> 71.9 us
  blocking collectives: 296 us -> 11.2 us
  starting transfers between devices: 69.9 us -> 13.9 us
  other arithmetic: 50.9 us -> 0 us
  between operations: 23.3 us -> 0.7 us
  local copies, waits for them, and re-layouts: 24 us -> 3.44 us
  waiting for transfers between devices: 45.1 us -> 24.9 us
  Pallas kernels: 0 us -> 17.1 us
  matrix products: 10.1 us -> 0.72 us
    psum x6 -> x0, blocking collectives: 252 us -> none  [inner_pair(): lax.psum((jnp.sum(first * first), jnp.sum(first * second)), ('gx', 'sp'))]
    ppermute x30 -> x8, starting transfers between devices: 66.4 us -> 11.3 us  [shifted(): lax.ppermute(array, axis, [(i, (i + amount) % count) for i in range(count)])]
    mul x8 -> x0, other arithmetic: 37.9 us -> none  [the longest x2 14.8 us: solve_system(): factor[i][j] = running * inverse[j]]
    all_gather x2 -> x0, blocking collectives: 27.2 us -> none  [the longest x1 13.7 us: per_device(): lax.all_gather(conduct, 'sp', axis=2, tiled=True)]
    pallas_call x0 -> x5, Pallas kernels: none -> 17.1 us  [call(): pl.pallas_call(kernel, out_shape=shapes, in_specs=[smem] * len(tables) +...]
    ppermute x30 -> x8, waiting for transfers between devices: 34.6 us -> 19.1 us  [shifted(): lax.ppermute(array, axis, [(i, (i + amount) % count) for i in range(count)])]
    dot_general x6 -> x1, matrix products: 10.1 us -> 0.72 us  [per_device(): jnp.dot(stoich.T, stoich, precision=lax.Precision.HIGHEST, preferred_elem...]
    unnamed x38 -> x21, local copies, waits for them, and re-layouts: 12.7 us -> 3.44 us
  transfers between devices with their start and end apart: 31 -> 9, of which waited for: 17 -> 4; matrix products, arithmetic and copies ran while one was open for 0% -> 2% of each run, Pallas kernels for 0% -> 0%
where the time goes in v1:
time: 72.2 us; the launch traced here: 71.9 us
  waiting for transfers between devices  24.9 us (34%)
  Pallas kernels  17.1 us (24%)
  starting transfers between devices  13.9 us (19%)
  blocking collectives  11.2 us (16%)
  local copies, waits for them, and re-layouts  3.44 us (5%)
    ppermute x8, waiting for transfers between devices, shifted(): lax.ppermute(array, axis, [(i, (i + amount) % count) for i in range(count)])  19.1 us
    pallas_call x5, Pallas kernels, call(): pl.pallas_call(kernel, out_shape=shapes, in_specs=[smem] * len(tables) +...  17.1 us
    ppermute x8, starting transfers between devices, shifted(): lax.ppermute(array, axis, [(i, (i + amount) % count) for i in range(count)])  11.3 us
    all_to_all x1, blocking collectives, per_device(): stats = lax.all_to_all(stats, ('gx', 'sp'), 0, 0, tiled=True)  11.2 us
    all_to_all x1, waiting for transfers between devices, per_device(): sums = lax.all_to_all(sums, ('gx', 'sp'), 0, 0, tiled=True)  5.72 us
    unnamed x21, local copies, waits for them, and re-layouts  3.44 us
    all_to_all x1, starting transfers between devices, per_device(): sums = lax.all_to_all(sums, ('gx', 'sp'), 0, 0, tiled=True)  2.54 us
  transfers between devices with their start and end apart: 9, of which 4 were waited for; matrix products, arithmetic and copies ran while one was open for 2% of the time, Pallas kernels for 0%

profile of v1, /device:TPU:0, one launch (start us, length us, event | category | flops | bytes accessed | tf_op | source)
XLA Modules:
  0.0 71.9 jit_solution(12746385273248946487)
XLA Ops:
  0.6 2.1 %shard_map.113 = (f32[25,8,128]{2,1,0:T(8,128)}, f32[41,8,128]{2,1,0:T(8,128)}, f32[25,8,128]{2,1,0:T(8,128)}, f32[41,8,128]{2,1,0:T(8,128)}, f32[32,128]{1,0:T(8,128)}) custom-call(f32[8]{0:T(128)} %cond_t.3, f32[8]{0:T(128)} %store_t.5, f32[8,8,128]{2,1,0:T(8,128)} %previous.1, f32[8,8,128]{2,1,0:T(8,128)} %recharge.1, s32[8,8,128]{2,1,0:T(8,128)} %zone.1, ...), custom_call_target="tpu_custom_call" | custom-call | tf_op jit(solution)/shard_map/pallas_call | solution.py:394
  2.7 5.1 %collective-permute-start.2 = (f32[41,8,128]{2,1,0:T(8,128)}, f32[41,8,128]{2,1,0:T(8,128)S(1)}, u32[]{:S(2)}, u32[]{:S(2)}) collective-permute-start(f32[41,8,128]{2,1,0:T(8,128)} %get-tuple-element.23), channel_id=1, source_target_pairs={{0,3},{1,0},{2,1},{3,2},{4,7},{5,4},{6,5},{7,6},{8,11},{9,8},{10,9... | collective-permute-start | bytes 503816 | tf_op jit(solution)/shard_map/ppermute | solution.py:405
  7.8 1.0 %collective-permute-start.1 = (f32[25,8,128]{2,1,0:T(8,128)}, f32[25,8,128]{2,1,0:T(8,128)S(1)}, u32[]{:S(2)}, u32[]{:S(2)}) collective-permute-start(f32[25,8,128]{2,1,0:T(8,128)} %get-tuple-element.22), channel_id=1, source_target_pairs={{0,2},{1,3},{2,0},{3,1},{4,6},{5,7},{6,4},{7,5},{8,10},{9,11},{10,... | collective-permute-start | bytes 307208 | tf_op jit(solution)/shard_map/ppermute | solution.py:405
  8.8 10.6 %collective-permute-done.1.refs_2_ = f32[25,8,128]{2,1,0:T(8,128)S(1)} collective-permute-done((f32[25,8,128]{2,1,0:T(8,128)}, f32[25,8,128]{2,1,0:T(8,128)S(1)}, u32[]{:S(2)}, u32[]{:S(2)}) %collective-permute-start.1) | collective-permute-done | bytes 102432 | tf_op jit(solution)/shard_map/ppermute | solution.py:405
  19.5 0.6 copy-done.4
  20.1 0.1 copy-done.2
  20.2 2.0 %shard_map.114 = (f32[44,8,128]{2,1,0:T(8,128)}, f32[44,8,128]{2,1,0:T(8,128)}) custom-call(f32[41,8,128]{2,1,0:T(8,128)} %get-tuple-element.20.own_field, f32[25,8,128]{2,1,0:T(8,128)} %get-tuple-element.21.refs_0_, f32[41,8,128]{2,1,0:T(8,128)} %copy-done.3, f32[25,8,128]{2,1,0:T(8,128)} %copy-done.4, f32[41,8,128]{2,1,0:T(8,128)} %copy-done.2), custom_call_target="tpu_custom_call" | custom-call | tf_op jit(solution)/shard_map/pallas_call | solution.py:394
  22.2 2.6 %collective-permute-start.4 = (f32[44,8,128]{2,1,0:T(8,128)}, f32[44,8,128]{2,1,0:T(8,128)S(1)}, u32[]{:S(2)}, u32[]{:S(2)}) collective-permute-start(f32[44,8,128]{2,1,0:T(8,128)} %get-tuple-element.24.own), channel_id=1, source_target_pairs={{0,28},{4,0},{8,4},{12,8},{16,12},{20,16},{24,20},{28,24},{1,29},{... | collective-permute-start | bytes 540680 | tf_op jit(solution)/shard_map/ppermute | solution.py:405
  24.8 11.2 %all_to_all.22 = f32[32,1,128]{2,1,0:T(1,128)} all-to-all(f32[32,1,128]{2,1,0:T(1,128)} %bitcast.13), channel_id=1, replica_groups=mesh['gx'=8,'sp'=4] {'gx','sp'}, dimensions={0} | all-to-all | bytes 32768 | tf_op jit(solution)/shard_map/all_to_all | solution.py:437
  36.1 0.7 copy-done
  36.8 3.9 %shard_map.115 = (f32[7,8,24,256]{3,2,1,0:T(8,128)}, f32[8,24,256]{2,1,0:T(8,128)}, f32[8,24,256]{2,1,0:T(8,128)}, f32[9,24,256]{2,1,0:T(8,128)}, f32[32,128]{1,0:T(8,128)}) custom-call(f32[8]{0:T(128)} %cond_t.3, f32[8]{0:T(128)} %store_t.5, f32[32,128]{1,0:T(8,128)} %bitcast.10, f32[44,8,128]{2,1,0:T(8,128)} %get-tuple-element.24.own, ...), custom_call_target="tpu_custom_call" | custom-call | tf_op jit(solution)/shard_map/pallas_call | solution.py:394
  40.7 2.5 %all-to-all-start.1 = ((f32[32,1,128]{2,1,0:T(1,128)}), f32[32,1,128]{2,1,0:T(1,128)S(1)}, u32[]{:S(2)}, u32[]{:S(2)}) async-start(f32[32,1,128]{2,1,0:T(1,128)} %bitcast.14), calls=%async_computation.1 | async-start | bytes 32768 | tf_op jit(solution)/shard_map/all_to_all | solution.py:451
  43.3 0.7 %fusion.powers = f32[8,8]{1,0:T(8,128)} fusion(f32[12,8]{0,1:T(8,128)S(1)} %copy-done.9), kind=kOutput, calls=%fused_computation | convolution fusion | flops 9216 | bytes 640 | tf_op jit(solution)/shard_map/dot_general | solution.py:452
  44.0 0.7 copy.15.stoich
  44.7 5.7 %all-to-all-done.1 = f32[32,1,128]{2,1,0:T(1,128)S(1)} async-done(((f32[32,1,128]{2,1,0:T(1,128)}), f32[32,1,128]{2,1,0:T(1,128)S(1)}, u32[]{:S(2)}, u32[]{:S(2)}) %all-to-all-start.1) | async-done | bytes 16416 | tf_op jit(solution)/shard_map/all_to_all | solution.py:451
  50.4 0.6 copy-done.8
  51.0 7.3 %shard_map.116 = (f32[8,8,128]{2,1,0:T(8,128)}, f32[24,8,128]{2,1,0:T(8,128)}, f32[24,8,128]{2,1,0:T(8,128)}, f32[24,8,128]{2,1,0:T(8,128)}, f32[24,8,128]{2,1,0:T(8,128)}) custom-call(f32[8]{0:T(128)} %store_t.5, f32[6,8]{1,0:T(8,128)} %rate_t.1, f32[12,8]{1,0:T(8,128)} %copy.15.stoich, f32[8,8]{1,0:T(8,128)} %fusion.powers, f32[8]{0:T(128)} %log_equil.1, ...), custom_call_target="tpu_custom_call" | custom-call | tf_op jit(solution)/shard_map/pallas_call | solution.py:394
  58.2 0.6 collective-permute-start.5
  58.8 1.4 %collective-permute-start.6 = (f32[24,8,128]{2,1,0:T(8,128)}, f32[24,8,128]{2,1,0:T(8,128)S(1)}, u32[]{:S(2)}, u32[]{:S(2)}) collective-permute-start(f32[24,8,128]{2,1,0:T(8,128)} %get-tuple-element.34), channel_id=1, source_target_pairs={{0,2},{1,3},{2,0},{3,1},{4,6},{5,7},{6,4},{7,5},{8,10},{9,11},{10,... | collective-permute-start | bytes 294920 | tf_op jit(solution)/shard_map/ppermute | solution.py:405
  60.2 0.6 collective-permute-start.7
  60.8 2.8 %collective-permute-done.5.refs_1_ = f32[24,8,128]{2,1,0:T(8,128)S(1)} collective-permute-done((f32[24,8,128]{2,1,0:T(8,128)}, f32[24,8,128]{2,1,0:T(8,128)S(1)}, u32[]{:S(2)}, u32[]{:S(2)}) %collective-permute-start.5) | collective-permute-done | bytes 98336 | tf_op jit(solution)/shard_map/ppermute | solution.py:405
  63.7 5.7 %collective-permute-done.6.refs_2_ = f32[24,8,128]{2,1,0:T(8,128)S(1)} collective-permute-done((f32[24,8,128]{2,1,0:T(8,128)}, f32[24,8,128]{2,1,0:T(8,128)S(1)}, u32[]{:S(2)}, u32[]{:S(2)}) %collective-permute-start.6) | collective-permute-done | bytes 98336 | tf_op jit(solution)/shard_map/ppermute | solution.py:405
  69.4 0.6 copy-done.6
  70.0 1.8 %shard_map.117 = f32[3,8,8,512]{3,2,1,0:T(8,128)} custom-call(f32[24,8,128]{2,1,0:T(8,128)} %get-tuple-element.32.refs_0_, f32[24,8,128]{2,1,0:T(8,128)} %copy-done.5, f32[24,8,128]{2,1,0:T(8,128)} %copy-done.6, f32[24,8,128]{2,1,0:T(8,128)} %copy-done.7), custom_call_target="tpu_custom_call" | custom-call | tf_op jit(solution)/shard_map/pallas_call | solution.py:394
  (22 shorter events, 0.2 us)
Async XLA Ops:
  0.6 42.6 %copy-start.9 = (f32[12,8]{0,1:T(8,128)S(1)}, f32[12,8]{0,1:T(8,128)}, u32[]{:S(2)}) copy-start(f32[12,8]{0,1:T(8,128)} %param.18) | copy-start | bytes 1156
  2.7 16.7 %collective-permute-start.2 = (f32[41,8,128]{2,1,0:T(8,128)}, f32[41,8,128]{2,1,0:T(8,128)S(1)}, u32[]{:S(2)}, u32[]{:S(2)}) collective-permute-start(f32[41,8,128]{2,1,0:T(8,128)} %get-tuple-element.23), channel_id=1, source_target_pairs={{0,3},{1,0},{2,1},{3,2},{4,7},{5,4},{6,5},{7,6},{8,11},{9,8},{10,9... | collective-permute-start | bytes 503816 | tf_op jit(solution)/shard_map/ppermute | solution.py:405
  7.8 11.6 %collective-permute-start = (f32[41,8,128]{2,1,0:T(8,128)}, f32[41,8,128]{2,1,0:T(8,128)S(1)}, u32[]{:S(2)}, u32[]{:S(2)}) collective-permute-start(f32[41,8,128]{2,1,0:T(8,128)} %get-tuple-element.20.own_field), channel_id=1, source_target_pairs={{0,1},{1,2},{2,3},{3,0},{4,5},{5,6},{6,7},{7,4},{8,9},{9,10},{10,1... | collective-permute-start | bytes 503816 | tf_op jit(solution)/shard_map/ppermute | solution.py:405
  7.8 11.6 %collective-permute-start.1 = (f32[25,8,128]{2,1,0:T(8,128)}, f32[25,8,128]{2,1,0:T(8,128)S(1)}, u32[]{:S(2)}, u32[]{:S(2)}) collective-permute-start(f32[25,8,128]{2,1,0:T(8,128)} %get-tuple-element.22), channel_id=1, source_target_pairs={{0,2},{1,3},{2,0},{3,1},{4,6},{5,7},{6,4},{7,5},{8,10},{9,11},{10,... | collective-permute-start | bytes 307208 | tf_op jit(solution)/shard_map/ppermute | solution.py:405
  19.4 0.6 copy-start.4
  19.4 0.7 copy-start.2
  19.5 0.8 %copy-start.3 = (f32[41,8,128]{2,1,0:T(8,128)}, f32[41,8,128]{2,1,0:T(8,128)S(1)}, u32[]{:S(2)}) copy-start(f32[41,8,128]{2,1,0:T(8,128)S(1)} %collective-permute-done.refs_1_) | copy-start | bytes 503812
  22.2 13.9 %collective-permute-start.3 = (f32[44,8,128]{2,1,0:T(8,128)}, f32[44,8,128]{2,1,0:T(8,128)S(1)}, u32[]{:S(2)}, u32[]{:S(2)}) collective-permute-start(f32[44,8,128]{2,1,0:T(8,128)} %get-tuple-element.25), channel_id=1, source_target_pairs={{0,4},{4,8},{8,12},{12,16},{16,20},{20,24},{24,28},{28,0},{1,5},{5... | collective-permute-start | bytes 540680 | tf_op jit(solution)/shard_map/ppermute | solution.py:405
  22.2 13.9 %collective-permute-start.4 = (f32[44,8,128]{2,1,0:T(8,128)}, f32[44,8,128]{2,1,0:T(8,128)S(1)}, u32[]{:S(2)}, u32[]{:S(2)}) collective-permute-start(f32[44,8,128]{2,1,0:T(8,128)} %get-tuple-element.24.own), channel_id=1, source_target_pairs={{0,28},{4,0},{8,4},{12,8},{16,12},{20,16},{24,20},{28,24},{1,29},{... | collective-permute-start | bytes 540680 | tf_op jit(solution)/shard_map/ppermute | solution.py:405
  36.1 0.7 copy-start
  36.1 0.7 %copy-start.1 = (f32[44,8,128]{2,1,0:T(8,128)}, f32[44,8,128]{2,1,0:T(8,128)S(1)}, u32[]{:S(2)}) copy-start(f32[44,8,128]{2,1,0:T(8,128)S(1)} %collective-permute-done.4.below) | copy-start | bytes 540676
  40.7 9.7 %all-to-all-start.1 = ((f32[32,1,128]{2,1,0:T(1,128)}), f32[32,1,128]{2,1,0:T(1,128)S(1)}, u32[]{:S(2)}, u32[]{:S(2)}) async-start(f32[32,1,128]{2,1,0:T(1,128)} %bitcast.14), calls=%async_computation.1 | async-start | bytes 32768 | tf_op jit(solution)/shard_map/all_to_all | solution.py:451
  50.4 0.6 copy-start.8
  58.2 5.4 %collective-permute-start.5 = (f32[24,8,128]{2,1,0:T(8,128)}, f32[24,8,128]{2,1,0:T(8,128)S(1)}, u32[]{:S(2)}, u32[]{:S(2)}) collective-permute-start(f32[24,8,128]{2,1,0:T(8,128)} %get-tuple-element.33), channel_id=1, source_target_pairs={{0,3},{1,0},{2,1},{3,2},{4,7},{5,4},{6,5},{7,6},{8,11},{9,8},{10,9... | collective-permute-start | bytes 294920 | tf_op jit(solution)/shard_map/ppermute | solution.py:405
  58.8 10.5 %collective-permute-start.6 = (f32[24,8,128]{2,1,0:T(8,128)}, f32[24,8,128]{2,1,0:T(8,128)S(1)}, u32[]{:S(2)}, u32[]{:S(2)}) collective-permute-start(f32[24,8,128]{2,1,0:T(8,128)} %get-tuple-element.34), channel_id=1, source_target_pairs={{0,2},{1,3},{2,0},{3,1},{4,6},{5,7},{6,4},{7,5},{8,10},{9,11},{10,... | collective-permute-start | bytes 294920 | tf_op jit(solution)/shard_map/ppermute | solution.py:405
  60.2 9.1 %collective-permute-start.7 = (f32[24,8,128]{2,1,0:T(8,128)}, f32[24,8,128]{2,1,0:T(8,128)S(1)}, u32[]{:S(2)}, u32[]{:S(2)}) collective-permute-start(f32[24,8,128]{2,1,0:T(8,128)} %get-tuple-element.35), channel_id=1, source_target_pairs={{0,1},{1,2},{2,3},{3,0},{4,5},{5,6},{6,7},{7,4},{8,9},{9,10},{10,1... | collective-permute-start | bytes 294920 | tf_op jit(solution)/shard_map/ppermute | solution.py:405
  63.7 5.7 %copy-start.5 = (f32[24,8,128]{2,1,0:T(8,128)}, f32[24,8,128]{2,1,0:T(8,128)S(1)}, u32[]{:S(2)}) copy-start(f32[24,8,128]{2,1,0:T(8,128)S(1)} %collective-permute-done.5.refs_1_) | copy-start | bytes 294916
  69.3 0.6 copy-start.6
  69.4 0.7 copy-start.7

commit v2 on v1

v2 whole, which is shorter than its diff:
```python
import functools

import jax
import jax.numpy as jnp
from jax import lax
from jax.experimental import pallas as pl
from jax.experimental.pallas import tpu as pltpu
from jax.sharding import PartitionSpec as P


ITERS = 6
NEWTON = 2

time_step = 0.05
dispersion = 0.5
reaction_span = 0.5
newton_damping = 0.5

LANES = 128
VMEM_BYTES = 16 * 1024 * 1024
WHOLE_VMEM_BYTES = 60 * 1024 * 1024
BASIS = ITERS + 1
HALO = ITERS + 1
PAIRS = [(i, j) for j in range(BASIS) for i in range(j + 1)]
PAIR_AT = {pair: at for at, pair in enumerate(PAIRS)}
PAIR_ROWS = -(-len(PAIRS) // 8) * 8


def harmonic(center, other):
    return 2.0 * center * other / jnp.maximum(center + other, 1e-30)


def pick(labels, table, first):
    value = jnp.zeros(labels.shape, jnp.float32)
    for level in range(table.shape[0]):
        value = jnp.where(labels == level + first, table[level], value)
    return value


def lane_ids(shape):
    return lax.broadcasted_iota(jnp.int32, shape, len(shape) - 1)


def fetch(pairs, sems):
    copies = [pltpu.make_async_copy(source, target, sems.at[at]) for at, (source, target) in enumerate(pairs)]
    for copy in copies:
        copy.start()
    for copy in copies:
        copy.wait()


def field_kernel(cond_h, store_h, previous_h, recharge_h, zone_h, field, sides, cond_t, store_t, previous, recharge, zone, sems):
    fetch(
        [(cond_h, cond_t), (store_h, store_t), (previous_h, previous), (recharge_h, recharge), (zone_h, zone)],
        sems,
    )
    count = lax.axis_size("sp")
    me = lax.axis_index("sp")
    layers = previous.shape[0]
    shape = previous.shape[1:]
    lane = lane_ids(shape)
    conduct, bound = [], []
    to_left = to_right = jnp.zeros(shape, jnp.float32)
    for z in range(layers):
        labels = zone[z]
        conduct.append(pick(labels, cond_t, 0))
        storage = pick(labels, store_t, 0)
        bound.append(storage)
        values = (storage * previous[z] + recharge[z], (labels + 1).astype(jnp.float32))
        for part, value in enumerate(values):
            at = part * layers + z
            field[at] = value
            here = jnp.logical_and(lane >= at * HALO, lane < (at + 1) * HALO)
            to_left = jnp.where(here, pltpu.roll(value, at * HALO, 1), to_left)
            to_right = jnp.where(here, pltpu.roll(value, (at + 1) * HALO % LANES, 1), to_right)
    power = jnp.zeros(shape, jnp.float32)
    upright = [harmonic(conduct[z], conduct[(z + 1) % layers]) for z in range(layers)]
    for z in range(layers):
        here = conduct[z]
        total = upright[z] + upright[z - 1]
        for axis in range(2):
            face = harmonic(here, pltpu.roll(here, 1, axis))
            total = total + face + pltpu.roll(face, shape[axis] - 1, axis)
        square = bound[z] + 2.0 * total
        square = square * square
        power = power + square * square
    column = jnp.sum(power, axis=0, keepdims=True) * (1.0 / (layers * shape[0]))
    top = jnp.broadcast_to(jnp.max(column, axis=1, keepdims=True), shape)
    for s in range(count):
        tile = jnp.where(me + 1 == s, to_right, jnp.where(me - 1 == s, to_left, 0.0))
        tile = jnp.where(lane >= 2 * layers * HALO, top, tile)
        for g in range(sides.shape[0] // count):
            sides[g * count + s] = tile


def pack_kernel(species, *blocks):
    count = len(blocks)
    me = lax.axis_index("sp")
    groups, layers, rows = species.shape[:3]
    shape = (rows, LANES)
    lane = lane_ids(shape)
    for d in range(count):
        here = jnp.bitwise_xor(me, d)
        sides = (lax.rem(here + count - 1, count), here, lax.rem(here + 1, count))
        at = [pl.ds(pl.multiple_of(i * LANES, LANES), LANES) for i in sides]
        edge = jnp.zeros(shape, jnp.float32)
        for c in range(groups):
            for z in range(layers):
                j = c * layers + z
                blocks[d][j] = species[c, z, :, at[1]]
                edge = jnp.where(lane == 2 * j, pltpu.roll(species[c, z, :, at[2]], 2 * j, 1), edge)
                edge = jnp.where(
                    lane == 2 * j + 1, pltpu.roll(species[c, z, :, at[0]], 2 * j + 2, 1), edge
                )
        blocks[d][groups * layers] = edge


def rim_kernel(groups, *refs):
    *blocks, _, up, down = refs
    rows = blocks[0].shape[1]
    layers = (blocks[0].shape[0] - 1) // groups
    for d, block in enumerate(blocks):
        for c in range(groups):
            at = pl.ds(c * layers, layers)
            up[d * groups + c] = block[at, 0, :]
            down[d * groups + c] = block[at, rows - 1, :]


def krylov_kernel(cond_t, store_t, sides, previous, recharge, zone, above, below, basis, kx, ky, kz, scale, sums, cond_s, store_s, pair_s):
    tall_count, count = lax.axis_size("gx"), lax.axis_size("sp")
    me, me_s = lax.axis_index("gx"), lax.axis_index("sp")
    layers, tall, wide = cond_s.shape
    rows = tall // 3
    lane = lane_ids((rows, LANES))
    tops = jnp.max(sides[...], axis=0)
    tops = jnp.max(jnp.where(lane >= 2 * layers * HALO, tops, 0.0), axis=0, keepdims=True)
    top = jnp.sqrt(jnp.sqrt(jnp.max(tops, axis=1, keepdims=True)))
    scale[...] = jnp.broadcast_to(4.0 / top, scale.shape)
    twice = jnp.broadcast_to(2.0 / top, (1, wide))
    fourth = jnp.broadcast_to(4.0 / top, (1, wide))

    for part, block in enumerate((above, None, below)):
        there = me + part - 1
        valid = jnp.logical_and(there >= 0, there < tall_count)
        there = jnp.clip(there, 0, tall_count - 1) * count
        keep = valid.astype(jnp.float32)
        keep_left = jnp.logical_and(valid, me_s > 0).astype(jnp.float32)
        keep_right = jnp.logical_and(valid, me_s < count - 1).astype(jnp.float32)
        left = sides[there + jnp.maximum(me_s - 1, 0)] * keep_left
        right = sides[there + jnp.minimum(me_s + 1, count - 1)] * keep_right
        at = slice(part * rows, (part + 1) * rows)
        for z in range(layers):
            near = []
            for j in (z, layers + z):
                value = jnp.where(lane < HALO, pltpu.roll(right, (LANES - j * HALO) % LANES, 1), 0.0)
                value = jnp.where(
                    lane >= LANES - HALO, pltpu.roll(left, LANES - (j + 1) * HALO, 1), value
                )
                near.append(value)
            if block is None:
                field, labels = None, zone[z] + 1
            else:
                field, labels = block[z] * keep, block[layers + z] * keep
            for half, (field, labels) in enumerate(((field, labels), near)):
                cols = slice(half * LANES, (half + 1) * LANES)
                storage = pick(labels, store_t, 1)
                if field is None:
                    field = storage * previous[z] + recharge[z]
                basis[0, z, at, cols] = field
                cond_s[z, at, cols] = pick(labels, cond_t, 1)
                store_s[z, at, cols] = storage
    kz[0] = jnp.zeros((tall, wide), jnp.float32)
    for z in range(layers):
        here = cond_s[z]
        kx[z] = harmonic(here, pltpu.roll(here, tall - 1, 0))
        ky[z] = harmonic(here, pltpu.roll(here, wide - 1, 1))
        if z + 1 < layers:
            kz[z + 1] = harmonic(here, cond_s[z + 1])

    def operate(k):
        flow = None
        for z in range(layers):
            value = basis[k, z]
            along_x = kx[z] * (value - pltpu.roll(value, tall - 1, 0))
            along_y = ky[z] * (value - pltpu.roll(value, wide - 1, 1))
            image = store_s[z] * value
            image = image + (along_x - pltpu.roll(along_x, 1, 0))
            image = image + (along_y - pltpu.roll(along_y, 1, 1))
            if z + 1 < layers:
                along_z = kz[z + 1] * (value - basis[k, z + 1])
                image = image + along_z
            if z:
                image = image - flow
            flow = along_z
            yield z, value, image

    for z, value, image in operate(0):
        basis[1, z] = image * twice - value

    def step(k, carry):
        for z, value, image in operate(k):
            basis[k + 1, z] = image * fourth - 2.0 * value - basis[k - 1, z]
        return carry

    lax.fori_loop(1, ITERS, step, 0)

    totals = [None] * len(PAIRS)
    for z in range(layers):
        values = [basis[k, z, rows : 2 * rows, :LANES] for k in range(BASIS)]
        for at, (i, j) in enumerate(PAIRS):
            term = values[i] * values[j]
            totals[at] = term if z == 0 else totals[at] + term
    pair_s[...] = jnp.zeros(pair_s.shape, jnp.float32)
    for at, total in enumerate(totals):
        pair_s[at : at + 1, :] = jnp.sum(total, axis=0, keepdims=True)
    full = jnp.sum(pair_s[...], axis=1, keepdims=True)
    lane = lane_ids(pair_s.shape)
    row = lax.broadcasted_iota(jnp.int32, pair_s.shape, 0)
    line = jnp.sum(jnp.where(lane == row, full, 0.0), axis=0, keepdims=True)
    sums[...] = jnp.broadcast_to(line, sums.shape)


def galerkin_weights(gram):
    def inner(i, j):
        return gram[PAIR_AT[(min(i, j), max(i, j))]]

    matrix = {}
    for i in range(ITERS):
        for j in range(i + 1):
            if j == 0:
                matrix[(i, j)] = 2.0 * (inner(i, 0) + inner(i, 1))
            else:
                matrix[(i, j)] = inner(i, j + 1) + inner(i, j - 1) + 2.0 * inner(i, j)
    least = [matrix[(i, i)] * 2e-7 for i in range(ITERS)]
    right = [inner(i, 0) for i in range(ITERS)]
    inverse = []
    for j in range(ITERS):
        pivot = matrix[(j, j)]
        good = pivot > least[j]
        inverse.append(jnp.where(good, 1.0 / jnp.where(good, pivot, 1.0), 0.0))
        for i in range(j + 1, ITERS):
            factor = matrix[(i, j)] * inverse[j]
            right[i] = right[i] - factor * right[j]
            for k in range(j + 1, i + 1):
                matrix[(i, k)] = matrix[(i, k)] - factor * matrix[(k, j)]
    for i in reversed(range(ITERS)):
        for k in range(i + 1, ITERS):
            right[i] = right[i] - matrix[(k, i)] * right[k]
        right[i] = right[i] * inverse[i]
    return right


def react(moved, rates, powers, stoich, rows, log_equil):
    minerals = len(rates)
    first = []
    for m in range(minerals):
        total = None
        for value, row in zip(moved, rows):
            term = stoich[row, m] * value
            total = term if total is None else total + term
        first.append(total - log_equil[m])
    shift = None
    for _ in range(NEWTON):
        if shift is None:
            affinity = first
        else:
            affinity = []
            for m in range(minerals):
                total = first[m]
                for n in range(minerals):
                    total = total - powers[m, n] * shift[n]
                affinity.append(total)
        tangent = [jnp.tanh(value) for value in affinity]
        gap = [reaction_span * rate * value for rate, value in zip(rates, tangent)]
        if shift is not None:
            gap = [value - past for value, past in zip(gap, shift)]
        root = [jnp.sqrt(reaction_span * rate * (1.0 - value * value)) for rate, value in zip(rates, tangent)]
        matrix = {}
        for i in range(minerals):
            for j in range(i + 1):
                entry = root[i] * root[j] * powers[i, j]
                matrix[(i, j)] = entry + 1.0 if i == j else entry
        right = []
        for i in range(minerals):
            total = None
            for j in range(minerals):
                term = powers[i, j] * gap[j]
                total = term if total is None else total + term
            right.append(root[i] * total)
        inverse = [None] * minerals
        for j in range(minerals):
            inverse[j] = lax.rsqrt(matrix[(j, j)])
            for i in range(j + 1, minerals):
                matrix[(i, j)] = matrix[(i, j)] * inverse[j]
            right[j] = right[j] * inverse[j]
            for i in range(j + 1, minerals):
                right[i] = right[i] - matrix[(i, j)] * right[j]
                for k in range(j + 1, i + 1):
                    matrix[(i, k)] = matrix[(i, k)] - matrix[(i, j)] * matrix[(k, j)]
        for i in reversed(range(minerals)):
            right[i] = right[i] * inverse[i]
            for k in range(i):
                right[k] = right[k] - matrix[(i, k)] * right[i]
        delta = [newton_damping * (g - e * w) for g, e, w in zip(gap, root, right)]
        shift = delta if shift is None else [past + step for past, step in zip(shift, delta)]
    result = []
    for value, row in zip(moved, rows):
        for m in range(minerals):
            value = value - stoich[row, m] * shift[m]
        result.append(value)
    return result


def finish_kernel(groups, rate_t, stoich, powers, log_equil, scale, sums, mineral, basis, kx, ky, kz, above, below, *refs):
    count = lax.axis_size("sp")
    blocks, (head_out, *outs, head_s, pair_s) = refs[:count], refs[count:]
    me = lax.axis_index("sp")
    layers, rows = head_out.shape[:2]
    tall, wide = head_s.shape[1:]

    total = jnp.sum(sums[...], axis=0, keepdims=True)
    lane = lane_ids(pair_s.shape)
    row = lax.broadcasted_iota(jnp.int32, pair_s.shape, 0)
    spread = jnp.sum(jnp.where(lane == row, total, 0.0), axis=1, keepdims=True)
    pair_s[...] = jnp.broadcast_to(spread, pair_s.shape)
    gram = [pair_s[at : at + 1, :] for at in range(len(PAIRS))]
    weights = [weight * scale[0:1, :] for weight in galerkin_weights(gram)]
    weights = [jnp.concatenate([weight] * (wide // LANES), axis=1) for weight in weights]
    for z in range(layers):
        value = weights[0] * basis[0, z]
        for k in range(1, ITERS):
            value = value + weights[k] * basis[k, z]
        head_s[z] = value
        head_out[z] = value[rows : 2 * rows, :LANES]

    shape = (rows, LANES)
    lane = lane_ids(shape)
    row = lax.broadcasted_iota(jnp.int32, shape, 0)
    center = slice(rows, 2 * rows)

    def layer(z, carry):
        before, after = jnp.maximum(z - 1, 0), jnp.minimum(z + 1, layers - 1)
        value = head_s[z, :, :LANES]
        face = kx[z, :, :LANES]
        flow = face * (value - pltpu.roll(value, tall - 1, 0))
        faces = [(face[center], flow[center])]
        faces.append((pltpu.roll(face, 1, 0)[center], -pltpu.roll(flow, 1, 0)[center]))
        value = head_s[z, center, :]
        face = ky[z, center, :]
        flow = face * (value - pltpu.roll(value, wide - 1, 1))
        faces.append((face[:, :LANES], flow[:, :LANES]))
        faces.append((pltpu.roll(face, 1, 1)[:, :LANES], -pltpu.roll(flow, 1, 1)[:, :LANES]))
        value = value[:, :LANES]
        for face, other in ((kz[z + 1, center, :LANES], after), (kz[z, center, :LANES], before)):
            faces.append((face, face * (value - head_s[other, center, :LANES])))
        outward = None
        inward = []
        for face, flow in faces:
            term = jnp.maximum(flow, 0.0) + dispersion * face
            outward = term if outward is None else outward + term
            inward.append(time_step * (dispersion * face - jnp.minimum(flow, 0.0)))
        stay = 1.0 - time_step * outward

        moved, table_rows = [], []
        for d, block in enumerate(blocks):
            group = jnp.bitwise_xor(me, d)
            edge = block[groups * layers]
            for c in range(groups):
                at = c * layers
                here = block[at + z]
                side = pltpu.roll(edge, LANES - 1 - 2 * (c * layers + z), 1)
                line = pl.ds(z, 1)
                edge_at = d * groups + c
                following = jnp.where(row == rows - 1, below[edge_at, line, :], pltpu.roll(here, rows - 1, 0))
                preceding = jnp.where(row == 0, above[edge_at, line, :], pltpu.roll(here, 1, 0))
                result = stay * here + inward[0] * following + inward[1] * preceding
                result = result + inward[2] * jnp.where(lane == LANES - 1, side, pltpu.roll(here, LANES - 1, 1))
                result = result + inward[3] * jnp.where(lane == 0, side, pltpu.roll(here, 1, 1))
                result = result + inward[4] * block[at + after] + inward[5] * block[at + before]
                moved.append(result)
                table_rows.append(group * groups + c)
        labels = mineral[z]
        rates = []
        for m in range(rate_t.shape[1]):
            rate = jnp.zeros(shape, jnp.float32)
            for level in range(rate_t.shape[0]):
                rate = jnp.where(labels == level, rate_t[level, m], rate)
            rates.append(rate)
        reacted = react(moved, rates, powers, stoich, table_rows, log_equil)
        for at, result in enumerate(reacted):
            outs[at // groups][(at % groups) * layers + z] = result
        return carry

    lax.fori_loop(0, layers, layer, 0)


def place_kernel(*refs):
    *blocks, out = refs
    me = lax.axis_index("sp")
    groups, layers = out.shape[:2]
    for d, block in enumerate(blocks):
        column = pl.multiple_of(jnp.bitwise_xor(me, d) * LANES, LANES)
        for c in range(groups):
            for z in range(layers):
                out[c, z, :, pl.ds(column, LANES)] = block[c * layers + z]


def call(kernel, tables, arrays, out_shapes, scratch=(), space=pltpu.VMEM, limit=VMEM_BYTES):
    smem = pl.BlockSpec(memory_space=pltpu.SMEM)
    vmem = pl.BlockSpec(memory_space=pltpu.VMEM)
    outside = pl.BlockSpec(memory_space=space)
    shapes = [jax.ShapeDtypeStruct(shape, jnp.float32) for shape in out_shapes]
    return pl.pallas_call(
        kernel,
        out_shape=shapes,
        in_specs=[smem] * len(tables) + [outside] * len(arrays),
        out_specs=[vmem] * len(shapes),
        scratch_shapes=[pltpu.VMEM(one, jnp.float32) if isinstance(one, tuple) else one for one in scratch],
        compiler_params=pltpu.CompilerParams(vmem_limit_bytes=limit),
        cost_estimate=pl.CostEstimate(flops=200_000_000, bytes_accessed=4_000_000, transcendentals=0),
    )(*tables, *arrays)


def shifted(array, axis, amount):
    count = lax.axis_size(axis)
    return lax.ppermute(array, axis, [(i, (i + amount) % count) for i in range(count)])


def swapped(array, axis, mask):
    count = lax.axis_size(axis)
    return lax.ppermute(array, axis, [(i, i ^ mask) for i in range(count)])


def per_device(
    previous_head,
    recharge,
    soil_zone,
    soil_cond,
    soil_store,
    species,
    mineral_zone,
    rate_table,
    stoich,
    log_equil,
):
    count = lax.axis_size("sp")
    devices = count * lax.axis_size("gx")
    layers, rows, columns = previous_head.shape
    groups = species.shape[0]
    assert columns == LANES and layers == 8 and rows == 8 and count & (count - 1) == 0
    assert 2 * layers * HALO < LANES and 2 * groups * layers <= LANES
    tile = (rows, LANES)
    everywhere = ("gx", "sp")

    field, sides = call(
        field_kernel,
        [],
        [soil_cond, soil_store, previous_head, recharge, soil_zone],
        [(2 * layers,) + tile, (devices,) + tile],
        [pltpu.SMEM(soil_cond.shape, jnp.float32), pltpu.SMEM(soil_store.shape, jnp.float32)]
        + [(layers,) + tile] * 2
        + [pltpu.VMEM((layers,) + tile, jnp.int32), pltpu.SemaphoreType.DMA((5,))],
        pltpu.HBM,
        WHOLE_VMEM_BYTES,
    )
    sides = lax.all_to_all(sides, everywhere, 0, 0, tiled=True)
    below = shifted(field, "gx", -1)
    above = shifted(field, "gx", 1)
    blocks = call(pack_kernel, [], [species], [(groups * layers + 1,) + tile] * count)
    arrived = {d: swapped(blocks[d], "sp", d) for d in range(count - 1, 0, -1)}
    blocks = [blocks[0]] + [arrived[d] for d in range(1, count)]
    extended = (layers, 3 * rows, 2 * LANES)
    basis, kx, ky, kz, scale, sums = call(
        krylov_kernel,
        [soil_cond, soil_store],
        [sides, previous_head, recharge, soil_zone, above, below],
        [(BASIS,) + extended, extended, extended, (layers + 1,) + extended[1:], tile, (devices, LANES)],
        [extended, extended, (PAIR_ROWS, LANES)],
    )
    sums = lax.all_to_all(sums, everywhere, 0, 0, tiled=True)
    rims = call(
        functools.partial(rim_kernel, groups), [], blocks + [scale], [(count * groups, layers, LANES)] * 2
    )
    below, above = shifted(rims[0], "gx", -1), shifted(rims[1], "gx", 1)
    powers = jnp.dot(stoich.T, stoich, precision=lax.Precision.HIGHEST, preferred_element_type=jnp.float32)
    head_field, *reacted = call(
        functools.partial(finish_kernel, groups),
        [rate_table, stoich, powers, log_equil],
        [scale, sums, mineral_zone, basis, kx, ky, kz, above, below] + blocks,
        [(layers,) + tile] + [(groups * layers,) + tile] * count,
        [extended, (PAIR_ROWS, LANES)],
    )
    arrived = {d: swapped(reacted[d], "sp", d) for d in range(count - 1, 0, -1)}
    (species_out,) = call(place_kernel, [], [reacted[0]] + [arrived[d] for d in range(1, count)], [species.shape])
    return (head_field, species_out)


def solution(mesh):
    in_specs = (
        P(None, "gx", "sp"),
        P(None, "gx", "sp"),
        P(None, "gx", "sp"),
        P(),
        P(),
        P("sp", None, "gx", None),
        P(None, "gx", "sp"),
        P(),
        P(),
        P(),
    )
    out_specs = (P(None, "gx", "sp"), P("sp", None, "gx", None))

    return jax.shard_map(per_device, mesh=mesh, in_specs=in_specs, out_specs=out_specs, check_vma=False)
```

time: 72.2 us -> 54.4 us (0.75)
  blocking collectives: 11.2 us -> 0 us
  starting transfers between devices: 13.9 us -> 24.2 us
  waiting for transfers between devices: 24.9 us -> 15.5 us
  Pallas kernels: 17.1 us -> 12.3 us
  local copies, waits for them, and re-layouts: 3.44 us -> 1.12 us
    ppermute x8 -> x4, waiting for transfers between devices: 19.1 us -> 4.8 us  [shifted(): lax.ppermute(array, axis, [(i, (i + amount) % count) for i in range(count)])]
    all_to_all x1 -> x0, blocking collectives: 11.2 us -> none  [per_device(): stats = lax.all_to_all(stats, ('gx', 'sp'), 0, 0, tiled=True)]
    ppermute x0 -> x6, starting transfers between devices: none -> 8.84 us  [swapped(): return lax.ppermute(array, axis, [(i, i ^ mask) for i in range(count)])]
    all_to_all x1 -> x2, starting transfers between devices: 2.54 us -> 11.1 us  [the longest x1 7.33 us: per_device(): sides = lax.all_to_all(sides, everywhere, 0, 0, tiled=True)]
    ppermute x8 -> x4, starting transfers between devices: 11.3 us -> 4.25 us  [shifted(): lax.ppermute(array, axis, [(i, (i + amount) % count) for i in range(count)])]
    ppermute x0 -> x6, waiting for transfers between devices: none -> 6.58 us  [swapped(): return lax.ppermute(array, axis, [(i, i ^ mask) for i in range(count)])]
    pallas_call x5 -> x6, Pallas kernels: 17.1 us -> 12.3 us  [call(): pl.pallas_call(kernel, out_shape=shapes, in_specs=[smem] * len(tables) +...]
    unnamed x21, local copies, waits for them, and re-layouts: 3.44 us -> 1.12 us
  transfers between devices with their start and end apart: 9 -> 12, of which waited for: 4 -> 5; matrix products, arithmetic and copies ran while one was open for 2% -> 0% of each run, Pallas kernels for 0% -> 6%
where the time goes in v2:
time: 54.4 us; the launch traced here: 54.1 us
  starting transfers between devices  24.2 us (44%)
  waiting for transfers between devices  15.5 us (28%)
  Pallas kernels  12.3 us (23%)
  local copies, waits for them, and re-layouts  1.12 us (2%)
  between operations  0.83 us (2%)
    pallas_call x6, Pallas kernels, call(): pl.pallas_call(kernel, out_shape=shapes, in_specs=[smem] * len(tables) +...  12.3 us
    ppermute x6, starting transfers between devices, swapped(): return lax.ppermute(array, axis, [(i, i ^ mask) for i in range(count)])  8.84 us
    all_to_all x1, starting transfers between devices, per_device(): sides = lax.all_to_all(sides, everywhere, 0, 0, tiled=True)  7.33 us
    ppermute x6, waiting for transfers between devices, swapped(): return lax.ppermute(array, axis, [(i, i ^ mask) for i in range(count)])  6.58 us
    ppermute x4, waiting for transfers between devices, shifted(): lax.ppermute(array, axis, [(i, (i + amount) % count) for i in range(count)])  4.8 us
    ppermute x4, starting transfers between devices, shifted(): lax.ppermute(array, axis, [(i, (i + amount) % count) for i in range(count)])  4.25 us
    all_to_all x1, waiting for transfers between devices, per_device(): sums = lax.all_to_all(sums, everywhere, 0, 0, tiled=True)  4.12 us
    all_to_all x1, starting transfers between devices, per_device(): sums = lax.all_to_all(sums, everywhere, 0, 0, tiled=True)  3.79 us
  transfers between devices with their start and end apart: 12, of which 5 were waited for; matrix products, arithmetic and copies ran while one was open for 0% of the time, Pallas kernels for 6%

profile of v2, /device:TPU:0, one launch (start us, length us, event | category | flops | bytes accessed | tf_op | source)
XLA Modules:
  0.0 54.1 jit_solution(12009809278855195210)
XLA Ops:
  0.7 1.8 %shard_map.113 = (f32[16,8,128]{2,1,0:T(8,128)}, f32[32,8,128]{2,1,0:T(8,128)}) custom-call(f32[8]{0:T(128)} %cond_t.1, f32[8]{0:T(128)} %store_t.1, f32[8,8,128]{2,1,0:T(8,128)} %previous.1, f32[8,8,128]{2,1,0:T(8,128)} %recharge.1, s32[8,8,128]{2,1,0:T(8,128)} %zone.1), custom_call_target="tpu_custom_call" | custom-call | flops 200000000 | bytes 4000000 | tf_op jit(solution)/shard_map/pallas_call | solution.py:413
  2.5 7.3 %all-to-all-start = ((f32[32,8,128]{2,1,0:T(8,128)}), f32[32,8,128]{2,1,0:T(8,128)S(1)}, u32[]{:S(2)}, u32[]{:S(2)}) async-start(f32[32,8,128]{2,1,0:T(8,128)} %get-tuple-element.21), calls=%async_computation | async-start | bytes 262144 | tf_op jit(solution)/shard_map/all_to_all | solution.py:466
  9.9 1.0 %copy-done.3 = f32[3,8,8,512]{3,2,1,0:T(8,128)S(1)} copy-done((f32[3,8,8,512]{3,2,1,0:T(8,128)S(1)}, f32[3,8,8,512]{3,2,1,0:T(8,128)}, u32[]{:S(2)}) %copy-start.3) | copy-done | bytes 393240
  10.9 0.3 shard_map.115
  11.2 1.8 %collective-permute-start.2 = (f32[25,8,128]{2,1,0:T(8,128)S(1)}, f32[25,8,128]{2,1,0:T(8,128)S(1)}, u32[]{:S(2)}, u32[]{:S(2)}) collective-permute-start(f32[25,8,128]{2,1,0:T(8,128)S(1)} %get-tuple-element.30), channel_id=1, source_target_pairs={{0,1},{1,0},{2,3},{3,2},{4,5},{5,4},{6,7},{7,6},{8,9},{9,8},{10,11... | collective-permute-start | bytes 307208 | tf_op jit(solution)/shard_map/ppermute | solution.py:431
  13.0 2.4 %collective-permute-start.3 = (f32[25,8,128]{2,1,0:T(8,128)S(1)}, f32[25,8,128]{2,1,0:T(8,128)S(1)}, u32[]{:S(2)}, u32[]{:S(2)}) collective-permute-start(f32[25,8,128]{2,1,0:T(8,128)S(1)} %get-tuple-element.31), channel_id=1, source_target_pairs={{0,2},{1,3},{2,0},{3,1},{4,6},{5,7},{6,4},{7,5},{8,10},{9,11},{10,... | collective-permute-start | bytes 307208 | tf_op jit(solution)/shard_map/ppermute | solution.py:431
  15.4 0.2 collective-permute-start.4
  15.6 1.5 %collective-permute-start.1 = (f32[16,8,128]{2,1,0:T(8,128)}, f32[16,8,128]{2,1,0:T(8,128)S(1)}, u32[]{:S(2)}, u32[]{:S(2)}) collective-permute-start(f32[16,8,128]{2,1,0:T(8,128)} %get-tuple-element.22), channel_id=1, source_target_pairs={{0,28},{4,0},{8,4},{12,8},{16,12},{20,16},{24,20},{28,24},{1,29},{... | collective-permute-start | bytes 196616 | tf_op jit(solution)/shard_map/ppermute | solution.py:426
  17.2 2.4 %collective-permute-done.1.below = f32[16,8,128]{2,1,0:T(8,128)S(1)} collective-permute-done((f32[16,8,128]{2,1,0:T(8,128)}, f32[16,8,128]{2,1,0:T(8,128)S(1)}, u32[]{:S(2)}, u32[]{:S(2)}) %collective-permute-start.1) | collective-permute-done | bytes 65568 | tf_op jit(solution)/shard_map/ppermute | solution.py:426
  19.6 2.4 %collective-permute-done.above = f32[16,8,128]{2,1,0:T(8,128)S(1)} collective-permute-done((f32[16,8,128]{2,1,0:T(8,128)}, f32[16,8,128]{2,1,0:T(8,128)S(1)}, u32[]{:S(2)}, u32[]{:S(2)}) %collective-permute-start) | collective-permute-done | bytes 65568 | tf_op jit(solution)/shard_map/ppermute | solution.py:426
  22.0 3.2 %shard_map.114 = (f32[7,8,24,256]{3,2,1,0:T(8,128)S(1)}, f32[8,24,256]{2,1,0:T(8,128)S(1)}, f32[8,24,256]{2,1,0:T(8,128)S(1)}, f32[9,24,256]{2,1,0:T(8,128)S(1)}...) custom-call(f32[8]{0:T(128)S(1)} %copy-done.7, f32[8]{0:T(128)S(1)} %copy-done.8, f32[32,8,128]{2,1,0:T(8,128)S(1)} %all-to-all-done.sides, ...), custom_call_target="tpu_custom_call" | custom-call | flops 200000000 | bytes 4000000 | tf_op jit(solution)/shard_map/pallas_call | solution.py:413
  25.2 3.8 %all-to-all-start.1 = ((f32[32,1,128]{2,1,0:T(1,128)}), f32[32,1,128]{2,1,0:T(1,128)S(1)}, u32[]{:S(2)}, u32[]{:S(2)}) async-start(f32[32,1,128]{2,1,0:T(1,128)} %bitcast.1), calls=%async_computation.1 | async-start | bytes 32768 | tf_op jit(solution)/shard_map/all_to_all | solution.py:480
  29.1 0.3 collective-permute-start.5
  29.4 2.4 %collective-permute-start.6 = (f32[12,8,128]{2,1,0:T(8,128)S(1)}, f32[12,8,128]{2,1,0:T(8,128)S(1)}, u32[]{:S(2)}, u32[]{:S(2)}) collective-permute-start(f32[12,8,128]{2,1,0:T(8,128)S(1)} %get-tuple-element.34), channel_id=1, source_target_pairs={{0,28},{4,0},{8,4},{12,8},{16,12},{20,16},{24,20},{28,24},{1,29},{... | collective-permute-start | bytes 147464 | tf_op jit(solution)/shard_map/ppermute | solution.py:426
  31.8 0.1 fusion.powers
  31.9 0.1 copy.14.stoich
  32.0 4.1 %all-to-all-done.1 = f32[32,1,128]{2,1,0:T(1,128)S(1)} async-done(((f32[32,1,128]{2,1,0:T(1,128)}), f32[32,1,128]{2,1,0:T(1,128)S(1)}, u32[]{:S(2)}, u32[]{:S(2)}) %all-to-all-start.1) | async-done | bytes 16416 | tf_op jit(solution)/shard_map/all_to_all | solution.py:480
  36.1 6.2 %shard_map.117 = (f32[8,8,128]{2,1,0:T(8,128)}, f32[24,8,128]{2,1,0:T(8,128)S(1)}, f32[24,8,128]{2,1,0:T(8,128)S(1)}, f32[24,8,128]{2,1,0:T(8,128)S(1)}, f32[24,8,128]{2,1,0:T(8,128)S(1)}) custom-call(f32[6,8]{1,0:T(8,128)S(1)} %copy-done.1, f32[12,8]{1,0:T(8,128)S(1)} %copy.14.stoich, f32[8,8]{1,0:T(8,128)S(1)} %fusion.powers, f32[8]{0:T(128)S(1)} %copy-done.2, ...), custom_call_target="tpu_custom_call" | custom-call | flops 200000000 | bytes 4000000 | tf_op jit(solution)/shard_map/pallas_call | solution.py:413
  42.3 0.5 collective-permute-start.7
  42.8 1.1 %collective-permute-start.8 = (f32[24,8,128]{2,1,0:T(8,128)S(1)}, f32[24,8,128]{2,1,0:T(8,128)S(1)}, u32[]{:S(2)}, u32[]{:S(2)}) collective-permute-start(f32[24,8,128]{2,1,0:T(8,128)S(1)} %get-tuple-element.38), channel_id=1, source_target_pairs={{0,2},{1,3},{2,0},{3,1},{4,6},{5,7},{6,4},{7,5},{8,10},{9,11},{10,... | collective-permute-start | bytes 294920 | tf_op jit(solution)/shard_map/ppermute | solution.py:431
  43.9 2.8 %collective-permute-start.9 = (f32[24,8,128]{2,1,0:T(8,128)S(1)}, f32[24,8,128]{2,1,0:T(8,128)S(1)}, u32[]{:S(2)}, u32[]{:S(2)}) collective-permute-start(f32[24,8,128]{2,1,0:T(8,128)S(1)} %get-tuple-element.39), channel_id=1, source_target_pairs={{0,3},{1,2},{2,1},{3,0},{4,7},{5,6},{6,5},{7,4},{8,11},{9,10},{10,... | collective-permute-start | bytes 294920 | tf_op jit(solution)/shard_map/ppermute | solution.py:431
  46.7 1.4 %collective-permute-done.7.refs_1_ = f32[24,8,128]{2,1,0:T(8,128)S(1)} collective-permute-done((f32[24,8,128]{2,1,0:T(8,128)S(1)}, f32[24,8,128]{2,1,0:T(8,128)S(1)}, u32[]{:S(2)}, u32[]{:S(2)}) %collective-permute-start.7) | collective-permute-done | bytes 98336 | tf_op jit(solution)/shard_map/ppermute | solution.py:431
  48.1 5.1 %collective-permute-done.8.refs_2_ = f32[24,8,128]{2,1,0:T(8,128)S(1)} collective-permute-done((f32[24,8,128]{2,1,0:T(8,128)S(1)}, f32[24,8,128]{2,1,0:T(8,128)S(1)}, u32[]{:S(2)}, u32[]{:S(2)}) %collective-permute-start.8) | collective-permute-done | bytes 98336 | tf_op jit(solution)/shard_map/ppermute | solution.py:431
  53.3 0.8 %shard_map.118 = f32[3,8,8,512]{3,2,1,0:T(8,128)} custom-call(f32[24,8,128]{2,1,0:T(8,128)S(1)} %get-tuple-element.36.refs_0_, f32[24,8,128]{2,1,0:T(8,128)S(1)} %collective-permute-done.7.refs_1_, f32[24,8,128]{2,1,0:T(8,128)S(1)} %collective-permute-done.8.refs_2_, f32[24,8,128]{2,1,0:T(8,128)S(1)} %collective-permute-done.9.refs_3_), custom_call_target="tpu_custom_call" | custom-call | flops 200000000 | bytes 4000000 | tf_op jit(solution)/shard_map/pallas_call | solution.py:413
  (28 shorter events, 0.1 us)
Async XLA Ops:
  0.6 21.3 %copy-start.8 = (f32[8]{0:T(128)S(1)}, f32[8]{0:T(128)}, u32[]{:S(2)}) copy-start(f32[8]{0:T(128)} %store_t.1) | copy-start | bytes 100
  0.6 21.3 %copy-start.7 = (f32[8]{0:T(128)S(1)}, f32[8]{0:T(128)}, u32[]{:S(2)}) copy-start(f32[8]{0:T(128)} %cond_t.1) | copy-start | bytes 100
  0.7 21.3 %copy-start.6 = (s32[8,8,128]{2,1,0:T(8,128)S(1)}, s32[8,8,128]{2,1,0:T(8,128)}, u32[]{:S(2)}) copy-start(s32[8,8,128]{2,1,0:T(8,128)} %zone.1) | copy-start | bytes 98308
  0.7 21.3 %copy-start.5 = (f32[8,8,128]{2,1,0:T(8,128)S(1)}, f32[8,8,128]{2,1,0:T(8,128)}, u32[]{:S(2)}) copy-start(f32[8,8,128]{2,1,0:T(8,128)} %recharge.1) | copy-start | bytes 98308
  0.7 21.3 %copy-start.4 = (f32[8,8,128]{2,1,0:T(8,128)S(1)}, f32[8,8,128]{2,1,0:T(8,128)}, u32[]{:S(2)}) copy-start(f32[8,8,128]{2,1,0:T(8,128)} %previous.1) | copy-start | bytes 98308
  2.5 29.3 %copy-start.9 = (f32[12,8]{0,1:T(8,128)S(1)}, f32[12,8]{0,1:T(8,128)}, u32[]{:S(2)}) copy-start(f32[12,8]{0,1:T(8,128)} %param.18) | copy-start | bytes 1156
  2.5 33.6 %copy-start = (s32[8,8,128]{2,1,0:T(8,128)S(1)}, s32[8,8,128]{2,1,0:T(8,128)}, u32[]{:S(2)}) copy-start(s32[8,8,128]{2,1,0:T(8,128)} %mineral.1) | copy-start | bytes 98308
  2.5 33.6 %copy-start.1 = (f32[6,8]{1,0:T(8,128)S(1)}, f32[6,8]{1,0:T(8,128)}, u32[]{:S(2)}) copy-start(f32[6,8]{1,0:T(8,128)} %rate_t.1) | copy-start | bytes 580
  2.5 33.6 %copy-start.2 = (f32[8]{0:T(128)S(1)}, f32[8]{0:T(128)}, u32[]{:S(2)}) copy-start(f32[8]{0:T(128)} %log_equil.1) | copy-start | bytes 100
  2.5 19.4 %all-to-all-start = ((f32[32,8,128]{2,1,0:T(8,128)}), f32[32,8,128]{2,1,0:T(8,128)S(1)}, u32[]{:S(2)}, u32[]{:S(2)}) async-start(f32[32,8,128]{2,1,0:T(8,128)} %get-tuple-element.21), calls=%async_computation | async-start | bytes 262144 | tf_op jit(solution)/shard_map/all_to_all | solution.py:466
  9.9 1.0 %copy-start.3 = (f32[3,8,8,512]{3,2,1,0:T(8,128)S(1)}, f32[3,8,8,512]{3,2,1,0:T(8,128)}, u32[]{:S(2)}) copy-start(f32[3,8,8,512]{3,2,1,0:T(8,128)} %species.1) | copy-start | bytes 1179652
  11.2 17.8 %collective-permute-start.2 = (f32[25,8,128]{2,1,0:T(8,128)S(1)}, f32[25,8,128]{2,1,0:T(8,128)S(1)}, u32[]{:S(2)}, u32[]{:S(2)}) collective-permute-start(f32[25,8,128]{2,1,0:T(8,128)S(1)} %get-tuple-element.30), channel_id=1, source_target_pairs={{0,1},{1,0},{2,3},{3,2},{4,5},{5,4},{6,7},{7,6},{8,9},{9,8},{10,11... | collective-permute-start | bytes 307208 | tf_op jit(solution)/shard_map/ppermute | solution.py:431
  13.0 16.0 %collective-permute-start.3 = (f32[25,8,128]{2,1,0:T(8,128)S(1)}, f32[25,8,128]{2,1,0:T(8,128)S(1)}, u32[]{:S(2)}, u32[]{:S(2)}) collective-permute-start(f32[25,8,128]{2,1,0:T(8,128)S(1)} %get-tuple-element.31), channel_id=1, source_target_pairs={{0,2},{1,3},{2,0},{3,1},{4,6},{5,7},{6,4},{7,5},{8,10},{9,11},{10,... | collective-permute-start | bytes 307208 | tf_op jit(solution)/shard_map/ppermute | solution.py:431
  15.4 13.6 %collective-permute-start.4 = (f32[25,8,128]{2,1,0:T(8,128)S(1)}, f32[25,8,128]{2,1,0:T(8,128)S(1)}, u32[]{:S(2)}, u32[]{:S(2)}) collective-permute-start(f32[25,8,128]{2,1,0:T(8,128)S(1)} %get-tuple-element.32), channel_id=1, source_target_pairs={{0,3},{1,2},{2,1},{3,0},{4,7},{5,6},{6,5},{7,4},{8,11},{9,10},{10,... | collective-permute-start | bytes 307208 | tf_op jit(solution)/shard_map/ppermute | solution.py:431
  15.6 4.0 %collective-permute-start.1 = (f32[16,8,128]{2,1,0:T(8,128)}, f32[16,8,128]{2,1,0:T(8,128)S(1)}, u32[]{:S(2)}, u32[]{:S(2)}) collective-permute-start(f32[16,8,128]{2,1,0:T(8,128)} %get-tuple-element.22), channel_id=1, source_target_pairs={{0,28},{4,0},{8,4},{12,8},{16,12},{20,16},{24,20},{28,24},{1,29},{... | collective-permute-start | bytes 196616 | tf_op jit(solution)/shard_map/ppermute | solution.py:426
  17.2 4.8 %collective-permute-start = (f32[16,8,128]{2,1,0:T(8,128)}, f32[16,8,128]{2,1,0:T(8,128)S(1)}, u32[]{:S(2)}, u32[]{:S(2)}) collective-permute-start(f32[16,8,128]{2,1,0:T(8,128)} %get-tuple-element.22), channel_id=1, source_target_pairs={{0,4},{4,8},{8,12},{12,16},{16,20},{20,24},{24,28},{28,0},{1,5},{5... | collective-permute-start | bytes 196616 | tf_op jit(solution)/shard_map/ppermute | solution.py:426
  25.2 10.9 %all-to-all-start.1 = ((f32[32,1,128]{2,1,0:T(1,128)}), f32[32,1,128]{2,1,0:T(1,128)S(1)}, u32[]{:S(2)}, u32[]{:S(2)}) async-start(f32[32,1,128]{2,1,0:T(1,128)} %bitcast.1), calls=%async_computation.1 | async-start | bytes 32768 | tf_op jit(solution)/shard_map/all_to_all | solution.py:480
  29.1 7.0 %collective-permute-start.5 = (f32[12,8,128]{2,1,0:T(8,128)S(1)}, f32[12,8,128]{2,1,0:T(8,128)S(1)}, u32[]{:S(2)}, u32[]{:S(2)}) collective-permute-start(f32[12,8,128]{2,1,0:T(8,128)S(1)} %get-tuple-element.33), channel_id=1, source_target_pairs={{0,4},{4,8},{8,12},{12,16},{16,20},{20,24},{24,28},{28,0},{1,5},{5... | collective-permute-start | bytes 147464 | tf_op jit(solution)/shard_map/ppermute | solution.py:426
  29.4 6.7 %collective-permute-start.6 = (f32[12,8,128]{2,1,0:T(8,128)S(1)}, f32[12,8,128]{2,1,0:T(8,128)S(1)}, u32[]{:S(2)}, u32[]{:S(2)}) collective-permute-start(f32[12,8,128]{2,1,0:T(8,128)S(1)} %get-tuple-element.34), channel_id=1, source_target_pairs={{0,28},{4,0},{8,4},{12,8},{16,12},{20,16},{24,20},{28,24},{1,29},{... | collective-permute-start | bytes 147464 | tf_op jit(solution)/shard_map/ppermute | solution.py:426
  42.3 5.8 %collective-permute-start.7 = (f32[24,8,128]{2,1,0:T(8,128)S(1)}, f32[24,8,128]{2,1,0:T(8,128)S(1)}, u32[]{:S(2)}, u32[]{:S(2)}) collective-permute-start(f32[24,8,128]{2,1,0:T(8,128)S(1)} %get-tuple-element.37), channel_id=1, source_target_pairs={{0,1},{1,0},{2,3},{3,2},{4,5},{5,4},{6,7},{7,6},{8,9},{9,8},{10,11... | collective-permute-start | bytes 294920 | tf_op jit(solution)/shard_map/ppermute | solution.py:431
  42.8 10.5 %collective-permute-start.8 = (f32[24,8,128]{2,1,0:T(8,128)S(1)}, f32[24,8,128]{2,1,0:T(8,128)S(1)}, u32[]{:S(2)}, u32[]{:S(2)}) collective-permute-start(f32[24,8,128]{2,1,0:T(8,128)S(1)} %get-tuple-element.38), channel_id=1, source_target_pairs={{0,2},{1,3},{2,0},{3,1},{4,6},{5,7},{6,4},{7,5},{8,10},{9,11},{10,... | collective-permute-start | bytes 294920 | tf_op jit(solution)/shard_map/ppermute | solution.py:431
  43.9 9.3 %collective-permute-start.9 = (f32[24,8,128]{2,1,0:T(8,128)S(1)}, f32[24,8,128]{2,1,0:T(8,128)S(1)}, u32[]{:S(2)}, u32[]{:S(2)}) collective-permute-start(f32[24,8,128]{2,1,0:T(8,128)S(1)} %get-tuple-element.39), channel_id=1, source_target_pairs={{0,3},{1,2},{2,1},{3,0},{4,7},{5,6},{6,5},{7,4},{8,11},{9,10},{10,... | collective-permute-start | bytes 294920 | tf_op jit(solution)/shard_map/ppermute | solution.py:431
